TPU v7x, 128 devices: a whole 4x4x4 slice. The times are simulated.
128 devices in a mesh: mem: 2 (over y_lo), gx: 8 (over x, core), gy: 8 (over z, y_hi).
Axes of the slice: x: 4, y: 4 (y_hi: 2, y_lo: 2; y = y_hi * 2 + y_lo), z: 4, core: 2. Of those that a mesh axis runs over, the one named last changes fastest.
Arguments:
- alpha: float32 [128, 2, 8, 32, 1024], P('mem', None, None, 'gy', 'gx'), may hold values from -6 to 6
- static_control: float32 [2, 8, 32, 1024], P(None, None, 'gy', 'gx'), may hold values from -6 to 6
- perturbations: bfloat16 [128, 2, 8, 32, 1024], P('mem', None, None, 'gy', 'gx'), may hold values from -6 to 6
- sigma: float32 [2, 8, 32, 1024], P(None, None, 'gy', 'gx'), may hold values from 0.5 to 2
- obs_coef: float32 [2, 8, 65536], P(None, None, ('gx', 'gy')), may hold values from -1.5 to 1.5
- interp_weights: float32 [4, 65536], P(None, ('gx', 'gy')), may hold values from 0.1 to 0.9
- obs_values: float32 [65536], P(('gx', 'gy')), may hold values from -6 to 6
- obs_weights: float32 [65536], P(('gx', 'gy')), may hold values from 0.5 to 4
- obs_tile: int32 [65536, 1], P(('gx', 'gy')), may hold values from 0 to 63; in each aligned block of 1024 rows (0 to 1023, 1024 to 2047, ...) at most 32 rows name the same one
- obs_cell: int32 [65536], P(('gx', 'gy')), may hold values from 0 to 2047
Outputs:
- alpha_out: float32 [128, 2, 8, 32, 1024], P('mem', None, None, 'gy', 'gx')
- static_out: float32 [2, 8, 32, 1024], P(None, None, 'gy', 'gx')
- increment: float32 [2, 8, 32, 1024], P(None, None, 'gy', 'gx')
Inputs may be any that keep to these rules, and one draw needn't show every extreme that they name: `obs_tile`: within the rows of one device no tile is named more than 32 times; in some devices' rows a tile is named exactly 32 times.
All inputs are finite; a program needn't handle non-finite values.
Results may differ from a plain program's by a relative error of at most 0.0003.
Values sent between devices are 32-bit elements; how exact they have to be, the bound alone decides.
A program may use at most 128 MiB of HBM per device.

v0:
```python
import math

import jax
import jax.numpy as jnp
from jax import lax
from jax.sharding import PartitionSpec as P

MEMBERS = 128
ITERS = 2


diffusion = 0.45
loc_gain = 4.0
ens_share = 0.8660254037844386
static_share = 0.5
descent = 0.2


def with_halo(cells, sides, width):
    for axis, dim in sides:
        count = lax.axis_size(axis)
        ends = count - 1
        head = lax.slice_in_dim(cells, 0, width, axis=dim)
        tail = lax.slice_in_dim(cells, cells.shape[dim] - width, cells.shape[dim], axis=dim)
        cells = jnp.concatenate(
            [
                lax.ppermute(tail, axis, [(i, (i + 1) % count) for i in range(ends)]),
                cells,
                lax.ppermute(head, axis, [((i + 1) % count, i) for i in range(ends)]),
            ],
            axis=dim,
        )
    return cells


def from_everyone(shard, axis):
    copies = jnp.broadcast_to(shard, (lax.axis_size(axis), *shard.shape))
    return lax.all_to_all(copies, axis, split_axis=0, concat_axis=0, tiled=True)


def of_everyone(shard, axis):
    everything = from_everyone(shard, axis)
    return jnp.sum(everything, axis=0)


def from_behind(block, axis, distance):
    devices = range(lax.axis_size(axis))
    route = [(i - distance, i) for i in devices if i - distance in devices]
    return lax.ppermute(block, axis, route)


def relax(grid_field, axis_pos, offset, extent):
    count_cells = grid_field.shape[axis_pos]
    profile = [1, 1, 1]
    profile[axis_pos] = count_cells
    placed = offset + lax.broadcasted_iota(jnp.int32, tuple(profile), axis_pos)
    inside = (placed >= 0) & (placed < extent)
    widths = [(0, 0)] * 3
    widths[axis_pos] = (1, 1)
    for repeat in range(4):
        padded = jnp.pad(grid_field, widths)
        lower = lax.slice_in_dim(padded, 0, count_cells, axis=axis_pos)
        upper = lax.slice_in_dim(padded, 2, count_cells + 2, axis=axis_pos)
        grid_field = jnp.where(
            inside, grid_field + diffusion * (lower + upper - 2.0 * grid_field), 0.0
        )
    return grid_field


def smooth(grid_field):
    lon_cells = grid_field.shape[2]
    extended = with_halo(grid_field, (("gx", 2),), 4)
    extended = relax(
        extended, 2, lax.axis_index("gx") * lon_cells - 4, lon_cells * lax.axis_size("gx")
    )
    grid_field = extended[:, :, 4 : 4 + lon_cells]
    for repeat in range(4):
        rimmed = with_halo(grid_field, (("gy", 1),), 1)
        grid_field = grid_field + diffusion * (rimmed[:, :-2] + rimmed[:, 2:] - 2.0 * grid_field)
    return loc_gain * grid_field


def per_device(
    alpha,
    static_control,
    perturbations,
    sigma,
    obs_coef,
    interp_weights,
    obs_values,
    obs_weights,
    obs_tile,
    obs_cell,
):
    members, variables, levels, lat_cells, lon_cells = alpha.shape
    channels = variables * levels
    ens_scale = ens_share / math.sqrt(MEMBERS - 1)
    obs_rows = obs_tile.shape[0]
    tile_count = lax.axis_size(("gx", "gy"))
    capacity = 2 * obs_rows // tile_count
    target = obs_tile[:, 0]
    onehot = (target[:, None] == lax.broadcasted_iota(jnp.int32, (1, tile_count), 1)).astype(
        jnp.int32
    )
    slot_rank = jnp.sum((jnp.cumsum(onehot, axis=0) - onehot) * onehot, axis=1)
    slot_index = target * capacity + slot_rank
    pieces = [
        obs_coef.reshape(channels, obs_rows),
        interp_weights,
        obs_cell.astype(jnp.float32)[None],
    ]
    pieces = pieces + [obs_values[None], obs_weights[None]]
    record = jnp.concatenate(pieces, 0)
    features = record.shape[0]
    buffer = jnp.zeros((features, tile_count * capacity), jnp.float32).at[:, slot_index].set(record)
    arrived = lax.all_to_all(
        buffer.reshape(features, tile_count, capacity),
        ("gx", "gy"),
        split_axis=1,
        concat_axis=1,
        tiled=True,
    )
    arrived = arrived.reshape(features, tile_count * capacity)
    coef_in = arrived[:channels]
    weights_in = arrived[channels : channels + 4]
    cell_in = arrived[channels + 4].astype(jnp.int32)
    fine_row = cell_in // (2 * lon_cells)
    fine_column = cell_in % (2 * lon_cells)
    base_index = fine_row // 2 * (lon_cells + 1) + fine_column // 2
    offsets = (0, 1, lon_cells + 1, lon_cells + 2)
    sigma_flat = sigma.reshape(channels, lat_cells, lon_cells)
    pert_flat = perturbations.reshape(members, channels, lat_cells, lon_cells)
    alpha_flat = alpha.reshape(members * channels, lat_cells, lon_cells)
    static_flat = static_control.reshape(channels, lat_cells, lon_cells)
    increment = jnp.zeros((channels, lat_cells, lon_cells), jnp.float32)
    for iteration in range(ITERS):
        smoothed = smooth(jnp.concatenate([alpha_flat, static_flat], 0))
        loc_members = smoothed[: members * channels].reshape(
            members, channels, lat_cells, lon_cells
        )
        partial_sum = jnp.sum(pert_flat.astype(jnp.float32) * loc_members, axis=0)
        ensemble = of_everyone(partial_sum, "mem")
        increment = (
            ens_scale * ensemble + static_share * sigma_flat * smoothed[members * channels :]
        )
        top_row = from_behind(increment[:, :1, :], "gy", -1)
        taller = jnp.concatenate([increment, top_row], 1)
        side_column = from_behind(taller[:, :, :1], "gx", -1)
        extended = jnp.concatenate([taller, side_column], 2).reshape(channels, -1)
        mapped = jnp.zeros(coef_in.shape, jnp.float32)
        for corner in range(4):
            mapped = mapped + weights_in[corner][None] * extended[:, base_index + offsets[corner]]
        model_obs = jnp.sum(coef_in * mapped, axis=0)
        residual = arrived[channels + 6] * (model_obs - arrived[channels + 5])
        spread = coef_in * residual[None]
        adjoint = jnp.zeros((channels, (lat_cells + 1) * (lon_cells + 1)), jnp.float32)
        for corner in range(4):
            adjoint = adjoint.at[:, base_index + offsets[corner]].add(
                weights_in[corner][None] * spread
            )
        adjoint = adjoint.reshape(channels, lat_cells + 1, lon_cells + 1)
        from_below = from_behind(adjoint[:, lat_cells:, :], "gy", 1)
        adjoint = adjoint[:, :lat_cells, :].at[:, :1, :].add(from_below)
        from_left = from_behind(adjoint[:, :, lon_cells:], "gx", 1)
        adjoint = adjoint[:, :, :lon_cells].at[:, :, :1].add(from_left)
        weighted_pert = (pert_flat.astype(jnp.float32) * adjoint[None]).reshape(
            members * channels, lat_cells, lon_cells
        )
        smoothed_back = smooth(jnp.concatenate([weighted_pert, sigma_flat * adjoint], 0))
        alpha_flat = alpha_flat - descent * (
            alpha_flat + ens_scale * smoothed_back[: members * channels]
        )
        static_flat = static_flat - descent * (
            static_flat + static_share * smoothed_back[members * channels :]
        )
    alpha_out = alpha_flat.reshape(members, variables, levels, lat_cells, lon_cells)
    static_out = static_flat.reshape(variables, levels, lat_cells, lon_cells)
    return (alpha_out, static_out, increment.reshape(variables, levels, lat_cells, lon_cells))


def solution(mesh):
    placed = (
        P("mem", None, None, "gy", "gx"),
        P(None, None, "gy", "gx"),
        P("mem", None, None, "gy", "gx"),
        P(None, None, "gy", "gx"),
        P(None, None, ("gx", "gy")),
        P(None, ("gx", "gy")),
        P(("gx", "gy")),
        P(("gx", "gy")),
        P(("gx", "gy"), None),
        P(("gx", "gy")),
    )
    return jax.shard_map(
        per_device,
        mesh=mesh,
        in_specs=placed,
        out_specs=(
            P("mem", None, None, "gy", "gx"),
            P(None, None, "gy", "gx"),
            P(None, None, "gy", "gx"),
        ),
        check_vma=False,
    )
```

profile of v0, /device:TPU:1, one launch (start us, length us, event | category | flops | bytes accessed | tf_op | source)
XLA Modules:
  0.0 833.6 jit_solution(10633047756386796119)
XLA Ops:
  44.5 18.0 %reduce-window.6 = s32[64,8,128]{2,1,0:T(8,128)S(1)} reduce-window(s32[64,8,128]{2,1,0:T(8,128)S(1)} %fusion.81, s32[]{:T(128)} %constant.171.clone.1), window={size=1x1x128 pad=0_0x0_0x127_0}, to_apply=%region_0.0 | reduce-window | flops 8323072 | bytes 524292 | tf_op jit(solution)/shard_map/reduce-window
  83.0 14.1 %all-to-all-start = ((f32[64,1,736]{2,1,0:T(1,128)}), f32[64,1,736]{2,1,0:T(1,128)S(1)}, u32[]{:S(2)}, u32[]{:S(2)}) async-start(f32[64,1,736]{2,1,0:T(1,128)} %reshape.721), calls=%async_computation | async-start | bytes 393216 | tf_op jit(solution)/shard_map/all_to_all | solution.py:116
  97.7 9.9 %all-to-all-done = f32[64,1,736]{2,1,0:T(1,128)S(1)} async-done(((f32[64,1,736]{2,1,0:T(1,128)}), f32[64,1,736]{2,1,0:T(1,128)S(1)}, u32[]{:S(2)}, u32[]{:S(2)}) %all-to-all-start) | async-done | bytes 188448 | tf_op jit(solution)/shard_map/all_to_all | solution.py:116
  127.7 15.3 %collective-permute-done.7 = f32[1040,1,128]{2,0,1:T(8,128)S(1)} collective-permute-done((f32[1040,1,128]{2,0,1:T(8,128)S(1)}, f32[1040,1,128]{2,0,1:T(8,128)S(1)}, u32[]{:S(2)}, u32[]{:S(2)}) %collective-permute-start.7) | collective-permute-done | bytes 532512 | tf_op jit(solution)/shard_map/ppermute | solution.py:29
  156.2 12.3 %collective-permute-done.9 = f32[1040,1,128]{2,0,1:T(8,128)S(1)} collective-permute-done((f32[1040,1,128]{2,0,1:T(8,128)S(1)}, f32[1040,1,128]{2,0,1:T(8,128)S(1)}, u32[]{:S(2)}, u32[]{:S(2)}) %collective-permute-start.9) | collective-permute-done | bytes 532512 | tf_op jit(solution)/shard_map/ppermute | solution.py:29
  224.7 12.0 %scatter_custom_fusion.1 = f32[16,645]{0,1:T(8,128)S(1)} fusion(s32[2048]{0:T(1024)} %bitcast.158, f32[2048,16]{1,0:T(8,128)} %copy.398, f32[]{:T(128)} %constant.173.clone.1), kind=kCustom, calls=%fused_computation.172 | custom fusion | flops 32768 | bytes 41792 | tf_op jit(solution)/shard_map/scatter-add | solution.py:158
  236.8 12.0 %scatter_fusion = f32[16,645]{0,1:T(8,128)S(1)} fusion(f32[16,645]{0,1:T(8,128)S(1)} %scatter_custom_fusion.1, s32[2048]{0:T(1024)S(1)} %bitcast.146, f32[2048,16]{1,0:T(8,128)} %copy.400), kind=kCustom, calls=%fused_computation.10 | custom fusion | flops 32768 | bytes 401408 | tf_op jit(solution)/shard_map/scatter-add | solution.py:158
  248.8 12.0 %scatter_fusion.1 = f32[16,645]{0,1:T(8,128)S(1)} fusion(f32[16,645]{0,1:T(8,128)S(1)} %scatter_fusion, s32[2048]{0:T(1024)S(1)} %bitcast.152, f32[2048,16]{1,0:T(8,128)} %copy.402), kind=kCustom, calls=%fused_computation.11 | custom fusion | flops 32768 | bytes 401408 | tf_op jit(solution)/shard_map/scatter-add | solution.py:158
  260.9 11.9 %scatter_fusion.2 = f32[16,645]{0,1:T(8,128)S(1)} fusion(f32[16,645]{0,1:T(8,128)S(1)} %scatter_fusion.1, s32[2048]{0:T(1024)S(1)} %bitcast.149, f32[2048,16]{1,0:T(8,128)S(1)} %copy.404), kind=kCustom, calls=%fused_computation.12 | custom fusion | flops 32768 | bytes 401408 | tf_op jit(solution)/shard_map/scatter-add | solution.py:158
  334.7 12.8 %collective-permute-done.17 = f32[1040,1,128]{2,0,1:T(8,128)S(1)} collective-permute-done((f32[1040,1,128]{2,0,1:T(8,128)S(1)}, f32[1040,1,128]{2,0,1:T(8,128)S(1)}, u32[]{:S(2)}, u32[]{:S(2)}) %collective-permute-start.17) | collective-permute-done | bytes 532512 | tf_op jit(solution)/shard_map/ppermute | solution.py:29
  351.0 9.3 %collective-permute-done.18 = f32[1040,1,128]{2,0,1:T(8,128)S(1)} collective-permute-done((f32[1040,1,128]{2,0,1:T(8,128)S(1)}, f32[1040,1,128]{2,0,1:T(8,128)S(1)}, u32[]{:S(2)}, u32[]{:S(2)}) %collective-permute-start.18) | collective-permute-done | bytes 532512 | tf_op jit(solution)/shard_map/ppermute | solution.py:27
  360.4 13.2 %collective-permute-done.19 = f32[1040,1,128]{2,0,1:T(8,128)S(1)} collective-permute-done((f32[1040,1,128]{2,0,1:T(8,128)S(1)}, f32[1040,1,128]{2,0,1:T(8,128)S(1)}, u32[]{:S(2)}, u32[]{:S(2)}) %collective-permute-start.19) | collective-permute-done | bytes 532512 | tf_op jit(solution)/shard_map/ppermute | solution.py:29
  379.7 10.4 %collective-permute-done.20 = f32[1040,1,128]{2,0,1:T(8,128)S(1)} collective-permute-done((f32[1040,1,128]{2,0,1:T(8,128)S(1)}, f32[1040,1,128]{2,0,1:T(8,128)S(1)}, u32[]{:S(2)}, u32[]{:S(2)}) %collective-permute-start.20) | collective-permute-done | bytes 532512 | tf_op jit(solution)/shard_map/ppermute | solution.py:27
  390.1 12.8 %collective-permute-done.21 = f32[1040,1,128]{2,0,1:T(8,128)S(1)} collective-permute-done((f32[1040,1,128]{2,0,1:T(8,128)S(1)}, f32[1040,1,128]{2,0,1:T(8,128)S(1)}, u32[]{:S(2)}, u32[]{:S(2)}) %collective-permute-start.21) | collective-permute-done | bytes 532512 | tf_op jit(solution)/shard_map/ppermute | solution.py:29
  406.8 9.6 %collective-permute-done.22 = f32[1040,1,128]{2,0,1:T(8,128)S(1)} collective-permute-done((f32[1040,1,128]{2,0,1:T(8,128)S(1)}, f32[1040,1,128]{2,0,1:T(8,128)S(1)}, u32[]{:S(2)}, u32[]{:S(2)}) %collective-permute-start.22) | collective-permute-done | bytes 532512 | tf_op jit(solution)/shard_map/ppermute | solution.py:27
  416.4 12.5 %collective-permute-done.23 = f32[1040,1,128]{2,0,1:T(8,128)S(1)} collective-permute-done((f32[1040,1,128]{2,0,1:T(8,128)S(1)}, f32[1040,1,128]{2,0,1:T(8,128)S(1)}, u32[]{:S(2)}, u32[]{:S(2)}) %collective-permute-start.23) | collective-permute-done | bytes 532512 | tf_op jit(solution)/shard_map/ppermute | solution.py:29
  474.3 11.6 %collective-permute-done.27 = f32[1040,1,128]{2,0,1:T(8,128)S(1)} collective-permute-done((f32[1040,1,128]{2,0,1:T(8,128)S(1)}, f32[1040,1,128]{2,0,1:T(8,128)S(1)}, u32[]{:S(2)}, u32[]{:S(2)}) %collective-permute-start.27) | collective-permute-done | bytes 532512 | tf_op jit(solution)/shard_map/ppermute | solution.py:29
  498.2 11.6 %collective-permute-done.29 = f32[1040,1,128]{2,0,1:T(8,128)S(1)} collective-permute-done((f32[1040,1,128]{2,0,1:T(8,128)S(1)}, f32[1040,1,128]{2,0,1:T(8,128)S(1)}, u32[]{:S(2)}, u32[]{:S(2)}) %collective-permute-start.29) | collective-permute-done | bytes 532512 | tf_op jit(solution)/shard_map/ppermute | solution.py:29
  513.1 9.5 %collective-permute-done.30 = f32[1040,1,128]{2,0,1:T(8,128)S(1)} collective-permute-done((f32[1040,1,128]{2,0,1:T(8,128)S(1)}, f32[1040,1,128]{2,0,1:T(8,128)S(1)}, u32[]{:S(2)}, u32[]{:S(2)}) %collective-permute-start.30) | collective-permute-done | bytes 532512 | tf_op jit(solution)/shard_map/ppermute | solution.py:27
  522.7 11.6 %collective-permute-done.31 = f32[1040,1,128]{2,0,1:T(8,128)S(1)} collective-permute-done((f32[1040,1,128]{2,0,1:T(8,128)S(1)}, f32[1040,1,128]{2,0,1:T(8,128)S(1)}, u32[]{:S(2)}, u32[]{:S(2)}) %collective-permute-start.31) | collective-permute-done | bytes 532512 | tf_op jit(solution)/shard_map/ppermute | solution.py:29
  537.5 10.1 %collective-permute-done.32 = f32[1040,1,128]{2,0,1:T(8,128)S(1)} collective-permute-done((f32[1040,1,128]{2,0,1:T(8,128)S(1)}, f32[1040,1,128]{2,0,1:T(8,128)S(1)}, u32[]{:S(2)}, u32[]{:S(2)}) %collective-permute-start.32) | collective-permute-done | bytes 532512 | tf_op jit(solution)/shard_map/ppermute | solution.py:27
  547.6 11.6 %collective-permute-done.33 = f32[1040,1,128]{2,0,1:T(8,128)S(1)} collective-permute-done((f32[1040,1,128]{2,0,1:T(8,128)S(1)}, f32[1040,1,128]{2,0,1:T(8,128)S(1)}, u32[]{:S(2)}, u32[]{:S(2)}) %collective-permute-start.33) | collective-permute-done | bytes 532512 | tf_op jit(solution)/shard_map/ppermute | solution.py:29
  630.6 12.0 %scatter_custom_fusion.5 = f32[16,645]{0,1:T(8,128)S(1)} fusion(s32[2048]{0:T(1024)} %bitcast.159, f32[2048,16]{1,0:T(8,128)} %copy.431, f32[]{:T(128)} %constant.173.clone.1), kind=kCustom, calls=%fused_computation.170 | custom fusion | flops 32768 | bytes 41792 | tf_op jit(solution)/shard_map/scatter-add | solution.py:158
  642.7 12.0 %scatter_fusion.3 = f32[16,645]{0,1:T(8,128)S(1)} fusion(f32[16,645]{0,1:T(8,128)S(1)} %scatter_custom_fusion.5, s32[2048]{0:T(1024)S(1)} %bitcast.147, f32[2048,16]{1,0:T(8,128)} %copy.432), kind=kCustom, calls=%fused_computation.14 | custom fusion | flops 32768 | bytes 401408 | tf_op jit(solution)/shard_map/scatter-add | solution.py:158
  654.7 12.0 %scatter_fusion.4 = f32[16,645]{0,1:T(8,128)S(1)} fusion(f32[16,645]{0,1:T(8,128)S(1)} %scatter_fusion.3, s32[2048]{0:T(1024)S(1)} %bitcast.153, f32[2048,16]{1,0:T(8,128)} %copy.433), kind=kCustom, calls=%fused_computation.15 | custom fusion | flops 32768 | bytes 401408 | tf_op jit(solution)/shard_map/scatter-add | solution.py:158
  666.8 11.7 %scatter_fusion.5 = f32[16,645]{0,1:T(8,128)S(1)} fusion(f32[16,645]{0,1:T(8,128)S(1)} %scatter_fusion.4, s32[2048]{0:T(1024)S(1)} %bitcast.150, f32[2048,16]{1,0:T(8,128)S(1)} %copy.434), kind=kCustom, calls=%fused_computation.16 | custom fusion | flops 32768 | bytes 401408 | tf_op jit(solution)/shard_map/scatter-add | solution.py:158
  740.7 12.5 %collective-permute-done.41 = f32[1040,1,128]{2,0,1:T(8,128)S(1)} collective-permute-done((f32[1040,1,128]{2,0,1:T(8,128)S(1)}, f32[1040,1,128]{2,0,1:T(8,128)S(1)}, u32[]{:S(2)}, u32[]{:S(2)}) %collective-permute-start.41) | collective-permute-done | bytes 532512 | tf_op jit(solution)/shard_map/ppermute | solution.py:29
  756.6 9.3 %collective-permute-done.42 = f32[1040,1,128]{2,0,1:T(8,128)S(1)} collective-permute-done((f32[1040,1,128]{2,0,1:T(8,128)S(1)}, f32[1040,1,128]{2,0,1:T(8,128)S(1)}, u32[]{:S(2)}, u32[]{:S(2)}) %collective-permute-start.42) | collective-permute-done | bytes 532512 | tf_op jit(solution)/shard_map/ppermute | solution.py:27
  766.0 11.6 %collective-permute-done.43 = f32[1040,1,128]{2,0,1:T(8,128)S(1)} collective-permute-done((f32[1040,1,128]{2,0,1:T(8,128)S(1)}, f32[1040,1,128]{2,0,1:T(8,128)S(1)}, u32[]{:S(2)}, u32[]{:S(2)}) %collective-permute-start.43) | collective-permute-done | bytes 532512 | tf_op jit(solution)/shard_map/ppermute | solution.py:29
  780.8 9.8 %collective-permute-done.44 = f32[1040,1,128]{2,0,1:T(8,128)S(1)} collective-permute-done((f32[1040,1,128]{2,0,1:T(8,128)S(1)}, f32[1040,1,128]{2,0,1:T(8,128)S(1)}, u32[]{:S(2)}, u32[]{:S(2)}) %collective-permute-start.44) | collective-permute-done | bytes 532512 | tf_op jit(solution)/shard_map/ppermute | solution.py:27
  790.7 12.7 %collective-permute-done.45 = f32[1040,1,128]{2,0,1:T(8,128)S(1)} collective-permute-done((f32[1040,1,128]{2,0,1:T(8,128)S(1)}, f32[1040,1,128]{2,0,1:T(8,128)S(1)}, u32[]{:S(2)}, u32[]{:S(2)}) %collective-permute-start.45) | collective-permute-done | bytes 532512 | tf_op jit(solution)/shard_map/ppermute | solution.py:29
  816.6 12.5 %collective-permute-done.47 = f32[1040,1,128]{2,0,1:T(8,128)S(1)} collective-permute-done((f32[1040,1,128]{2,0,1:T(8,128)S(1)}, f32[1040,1,128]{2,0,1:T(8,128)S(1)}, u32[]{:S(2)}, u32[]{:S(2)}) %collective-permute-start.47) | collective-permute-done | bytes 532512 | tf_op jit(solution)/shard_map/ppermute | solution.py:29
  (431 shorter events, 450.3 us)
Async XLA Ops:
  8.1 12.2 %collective-permute-start.1 = (f32[1040,4,4]{0,2,1:T(4,128)S(1)}, f32[1040,4,4]{0,2,1:T(4,128)S(1)}, u32[]{:S(2)}, u32[]{:S(2)}) collective-permute-start(f32[1040,4,4]{0,2,1:T(4,128)S(1)} %copy.377), channel_id=1, source_target_pairs={{8,0},{16,8},{24,16},{32,24},{40,32},{48,40},{56,48},{9,1},{17,9},... | collective-permute-start | bytes 199688 | tf_op jit(solution)/shard_map/ppermute | solution.py:29
  38.3 28.7 %collective-permute-start.2 = (f32[1040,1,128]{2,0,1:T(8,128)S(1)}, f32[1040,1,128]{2,0,1:T(8,128)S(1)}, u32[]{:S(2)}, u32[]{:S(2)}) collective-permute-start(f32[1040,1,128]{2,0,1:T(8,128)S(1)} %get-tuple-element.83), channel_id=1, source_target_pairs={{0,1},{1,2},{2,3},{3,4},{4,5},{5,6},{6,7},{8,9},{9,10},{10,11},{11... | collective-permute-start | bytes 1597448 | tf_op jit(solution)/shard_map/ppermute | solution.py:27
  43.1 24.5 %collective-permute-start.3 = (f32[1040,1,128]{2,0,1:T(8,128)S(1)}, f32[1040,1,128]{2,0,1:T(8,128)S(1)}, u32[]{:S(2)}, u32[]{:S(2)}) collective-permute-start(f32[1040,1,128]{2,0,1:T(8,128)S(1)} %get-tuple-element.84), channel_id=1, source_target_pairs={{1,0},{2,1},{3,2},{4,3},{5,4},{6,5},{7,6},{9,8},{10,9},{11,10},{12... | collective-permute-start | bytes 1597448 | tf_op jit(solution)/shard_map/ppermute | solution.py:29
  70.4 41.1 %collective-permute-start.4 = (f32[1040,1,128]{2,0,1:T(8,128)}, f32[1040,1,128]{2,0,1:T(8,128)}, u32[]{:S(2)}, u32[]{:S(2)}) collective-permute-start(f32[1040,1,128]{2,0,1:T(8,128)} %get-tuple-element.113), channel_id=1, source_target_pairs={{0,1},{1,2},{2,3},{3,4},{4,5},{5,6},{6,7},{8,9},{9,10},{10,11},{11... | collective-permute-start | bytes 1597448 | tf_op jit(solution)/shard_map/ppermute | solution.py:27
  76.1 35.4 %collective-permute-start.5 = (f32[1040,1,128]{2,0,1:T(8,128)}, f32[1040,1,128]{2,0,1:T(8,128)}, u32[]{:S(2)}, u32[]{:S(2)}) collective-permute-start(f32[1040,1,128]{2,0,1:T(8,128)} %get-tuple-element.114), channel_id=1, source_target_pairs={{1,0},{2,1},{3,2},{4,3},{5,4},{6,5},{7,6},{9,8},{10,9},{11,10},{12... | collective-permute-start | bytes 1597448 | tf_op jit(solution)/shard_map/ppermute | solution.py:29
  83.0 24.6 %all-to-all-start = ((f32[64,1,736]{2,1,0:T(1,128)}), f32[64,1,736]{2,1,0:T(1,128)S(1)}, u32[]{:S(2)}, u32[]{:S(2)}) async-start(f32[64,1,736]{2,1,0:T(1,128)} %reshape.721), calls=%async_computation | async-start | bytes 393216 | tf_op jit(solution)/shard_map/all_to_all | solution.py:116
  114.9 12.8 %collective-permute-start.6 = (f32[1040,1,128]{2,0,1:T(8,128)S(1)}, f32[1040,1,128]{2,0,1:T(8,128)S(1)}, u32[]{:S(2)}, u32[]{:S(2)}) collective-permute-start(f32[1040,1,128]{2,0,1:T(8,128)S(1)} %get-tuple-element.111), channel_id=1, source_target_pairs={{0,1},{1,2},{2,3},{3,4},{4,5},{5,6},{6,7},{8,9},{9,10},{10,11},{11... | collective-permute-start | bytes 1597448 | tf_op jit(solution)/shard_map/ppermute | solution.py:27
  117.1 26.0 %collective-permute-start.7 = (f32[1040,1,128]{2,0,1:T(8,128)S(1)}, f32[1040,1,128]{2,0,1:T(8,128)S(1)}, u32[]{:S(2)}, u32[]{:S(2)}) collective-permute-start(f32[1040,1,128]{2,0,1:T(8,128)S(1)} %get-tuple-element.112), channel_id=1, source_target_pairs={{1,0},{2,1},{3,2},{4,3},{5,4},{6,5},{7,6},{9,8},{10,9},{11,10},{12... | collective-permute-start | bytes 1597448 | tf_op jit(solution)/shard_map/ppermute | solution.py:29
  143.5 12.6 %collective-permute-start.8 = (f32[1040,1,128]{2,0,1:T(8,128)S(1)}, f32[1040,1,128]{2,0,1:T(8,128)S(1)}, u32[]{:S(2)}, u32[]{:S(2)}) collective-permute-start(f32[1040,1,128]{2,0,1:T(8,128)S(1)} %get-tuple-element.109), channel_id=1, source_target_pairs={{0,1},{1,2},{2,3},{3,4},{4,5},{5,6},{6,7},{8,9},{9,10},{10,11},{11... | collective-permute-start | bytes 1597448 | tf_op jit(solution)/shard_map/ppermute | solution.py:27
  146.1 22.4 %collective-permute-start.9 = (f32[1040,1,128]{2,0,1:T(8,128)S(1)}, f32[1040,1,128]{2,0,1:T(8,128)S(1)}, u32[]{:S(2)}, u32[]{:S(2)}) collective-permute-start(f32[1040,1,128]{2,0,1:T(8,128)S(1)} %get-tuple-element.110), channel_id=1, source_target_pairs={{1,0},{2,1},{3,2},{4,3},{5,4},{6,5},{7,6},{9,8},{10,9},{11,10},{12... | collective-permute-start | bytes 1597448 | tf_op jit(solution)/shard_map/ppermute | solution.py:29
  319.4 15.3 %collective-permute-start.16 = (f32[1040,1,128]{2,0,1:T(8,128)S(1)}, f32[1040,1,128]{2,0,1:T(8,128)S(1)}, u32[]{:S(2)}, u32[]{:S(2)}) collective-permute-start(f32[1040,1,128]{2,0,1:T(8,128)S(1)} %get-tuple-element.81), channel_id=1, source_target_pairs={{0,1},{1,2},{2,3},{3,4},{4,5},{5,6},{6,7},{8,9},{9,10},{10,11},{11... | collective-permute-start | bytes 1597448 | tf_op jit(solution)/shard_map/ppermute | solution.py:27
  324.9 22.7 %collective-permute-start.17 = (f32[1040,1,128]{2,0,1:T(8,128)S(1)}, f32[1040,1,128]{2,0,1:T(8,128)S(1)}, u32[]{:S(2)}, u32[]{:S(2)}) collective-permute-start(f32[1040,1,128]{2,0,1:T(8,128)S(1)} %get-tuple-element.82), channel_id=1, source_target_pairs={{1,0},{2,1},{3,2},{4,3},{5,4},{6,5},{7,6},{9,8},{10,9},{11,10},{12... | collective-permute-start | bytes 1597448 | tf_op jit(solution)/shard_map/ppermute | solution.py:29
  348.0 12.3 %collective-permute-start.18 = (f32[1040,1,128]{2,0,1:T(8,128)S(1)}, f32[1040,1,128]{2,0,1:T(8,128)S(1)}, u32[]{:S(2)}, u32[]{:S(2)}) collective-permute-start(f32[1040,1,128]{2,0,1:T(8,128)S(1)} %get-tuple-element.105), channel_id=1, source_target_pairs={{0,1},{1,2},{2,3},{3,4},{4,5},{5,6},{6,7},{8,9},{9,10},{10,11},{11... | collective-permute-start | bytes 1597448 | tf_op jit(solution)/shard_map/ppermute | solution.py:27
  349.7 23.8 %collective-permute-start.19 = (f32[1040,1,128]{2,0,1:T(8,128)S(1)}, f32[1040,1,128]{2,0,1:T(8,128)S(1)}, u32[]{:S(2)}, u32[]{:S(2)}) collective-permute-start(f32[1040,1,128]{2,0,1:T(8,128)S(1)} %get-tuple-element.106), channel_id=1, source_target_pairs={{1,0},{2,1},{3,2},{4,3},{5,4},{6,5},{7,6},{9,8},{10,9},{11,10},{12... | collective-permute-start | bytes 1597448 | tf_op jit(solution)/shard_map/ppermute | solution.py:29
  374.1 16.0 %collective-permute-start.20 = (f32[1040,1,128]{2,0,1:T(8,128)S(1)}, f32[1040,1,128]{2,0,1:T(8,128)S(1)}, u32[]{:S(2)}, u32[]{:S(2)}) collective-permute-start(f32[1040,1,128]{2,0,1:T(8,128)S(1)} %get-tuple-element.103), channel_id=1, source_target_pairs={{0,1},{1,2},{2,3},{3,4},{4,5},{5,6},{6,7},{8,9},{9,10},{10,11},{11... | collective-permute-start | bytes 1597448 | tf_op jit(solution)/shard_map/ppermute | solution.py:27
  378.4 24.4 %collective-permute-start.21 = (f32[1040,1,128]{2,0,1:T(8,128)S(1)}, f32[1040,1,128]{2,0,1:T(8,128)S(1)}, u32[]{:S(2)}, u32[]{:S(2)}) collective-permute-start(f32[1040,1,128]{2,0,1:T(8,128)S(1)} %get-tuple-element.104), channel_id=1, source_target_pairs={{1,0},{2,1},{3,2},{4,3},{5,4},{6,5},{7,6},{9,8},{10,9},{11,10},{12... | collective-permute-start | bytes 1597448 | tf_op jit(solution)/shard_map/ppermute | solution.py:29
  403.4 13.0 %collective-permute-start.22 = (f32[1040,1,128]{2,0,1:T(8,128)S(1)}, f32[1040,1,128]{2,0,1:T(8,128)S(1)}, u32[]{:S(2)}, u32[]{:S(2)}) collective-permute-start(f32[1040,1,128]{2,0,1:T(8,128)S(1)} %get-tuple-element.101), channel_id=1, source_target_pairs={{0,1},{1,2},{2,3},{3,4},{4,5},{5,6},{6,7},{8,9},{9,10},{10,11},{11... | collective-permute-start | bytes 1597448 | tf_op jit(solution)/shard_map/ppermute | solution.py:27
  405.4 23.5 %collective-permute-start.23 = (f32[1040,1,128]{2,0,1:T(8,128)S(1)}, f32[1040,1,128]{2,0,1:T(8,128)S(1)}, u32[]{:S(2)}, u32[]{:S(2)}) collective-permute-start(f32[1040,1,128]{2,0,1:T(8,128)S(1)} %get-tuple-element.102), channel_id=1, source_target_pairs={{1,0},{2,1},{3,2},{4,3},{5,4},{6,5},{7,6},{9,8},{10,9},{11,10},{12... | collective-permute-start | bytes 1597448 | tf_op jit(solution)/shard_map/ppermute | solution.py:29
  464.6 21.3 %collective-permute-start.27 = (f32[1040,1,128]{2,0,1:T(8,128)S(1)}, f32[1040,1,128]{2,0,1:T(8,128)S(1)}, u32[]{:S(2)}, u32[]{:S(2)}) collective-permute-start(f32[1040,1,128]{2,0,1:T(8,128)S(1)} %get-tuple-element.80), channel_id=1, source_target_pairs={{1,0},{2,1},{3,2},{4,3},{5,4},{6,5},{7,6},{9,8},{10,9},{11,10},{12... | collective-permute-start | bytes 1597448 | tf_op jit(solution)/shard_map/ppermute | solution.py:29
  487.9 21.9 %collective-permute-start.29 = (f32[1040,1,128]{2,0,1:T(8,128)S(1)}, f32[1040,1,128]{2,0,1:T(8,128)S(1)}, u32[]{:S(2)}, u32[]{:S(2)}) collective-permute-start(f32[1040,1,128]{2,0,1:T(8,128)S(1)} %get-tuple-element.98), channel_id=1, source_target_pairs={{1,0},{2,1},{3,2},{4,3},{5,4},{6,5},{7,6},{9,8},{10,9},{11,10},{12... | collective-permute-start | bytes 1597448 | tf_op jit(solution)/shard_map/ppermute | solution.py:29
  510.3 12.3 %collective-permute-start.30 = (f32[1040,1,128]{2,0,1:T(8,128)S(1)}, f32[1040,1,128]{2,0,1:T(8,128)S(1)}, u32[]{:S(2)}, u32[]{:S(2)}) collective-permute-start(f32[1040,1,128]{2,0,1:T(8,128)S(1)} %get-tuple-element.95), channel_id=1, source_target_pairs={{0,1},{1,2},{2,3},{3,4},{4,5},{5,6},{6,7},{8,9},{9,10},{10,11},{11... | collective-permute-start | bytes 1597448 | tf_op jit(solution)/shard_map/ppermute | solution.py:27
  511.8 22.4 %collective-permute-start.31 = (f32[1040,1,128]{2,0,1:T(8,128)S(1)}, f32[1040,1,128]{2,0,1:T(8,128)S(1)}, u32[]{:S(2)}, u32[]{:S(2)}) collective-permute-start(f32[1040,1,128]{2,0,1:T(8,128)S(1)} %get-tuple-element.96), channel_id=1, source_target_pairs={{1,0},{2,1},{3,2},{4,3},{5,4},{6,5},{7,6},{9,8},{10,9},{11,10},{12... | collective-permute-start | bytes 1597448 | tf_op jit(solution)/shard_map/ppermute | solution.py:29
  534.7 12.9 %collective-permute-start.32 = (f32[1040,1,128]{2,0,1:T(8,128)S(1)}, f32[1040,1,128]{2,0,1:T(8,128)S(1)}, u32[]{:S(2)}, u32[]{:S(2)}) collective-permute-start(f32[1040,1,128]{2,0,1:T(8,128)S(1)} %get-tuple-element.93), channel_id=1, source_target_pairs={{0,1},{1,2},{2,3},{3,4},{4,5},{5,6},{6,7},{8,9},{9,10},{10,11},{11... | collective-permute-start | bytes 1597448 | tf_op jit(solution)/shard_map/ppermute | solution.py:27
  536.2 23.0 %collective-permute-start.33 = (f32[1040,1,128]{2,0,1:T(8,128)S(1)}, f32[1040,1,128]{2,0,1:T(8,128)S(1)}, u32[]{:S(2)}, u32[]{:S(2)}) collective-permute-start(f32[1040,1,128]{2,0,1:T(8,128)S(1)} %get-tuple-element.94), channel_id=1, source_target_pairs={{1,0},{2,1},{3,2},{4,3},{5,4},{6,5},{7,6},{9,8},{10,9},{11,10},{12... | collective-permute-start | bytes 1597448 | tf_op jit(solution)/shard_map/ppermute | solution.py:29
  725.4 15.3 %collective-permute-start.40 = (f32[1040,1,128]{2,0,1:T(8,128)S(1)}, f32[1040,1,128]{2,0,1:T(8,128)S(1)}, u32[]{:S(2)}, u32[]{:S(2)}) collective-permute-start(f32[1040,1,128]{2,0,1:T(8,128)S(1)} %get-tuple-element.77), channel_id=1, source_target_pairs={{0,1},{1,2},{2,3},{3,4},{4,5},{5,6},{6,7},{8,9},{9,10},{10,11},{11... | collective-permute-start | bytes 1597448 | tf_op jit(solution)/shard_map/ppermute | solution.py:27
  730.9 22.3 %collective-permute-start.41 = (f32[1040,1,128]{2,0,1:T(8,128)S(1)}, f32[1040,1,128]{2,0,1:T(8,128)S(1)}, u32[]{:S(2)}, u32[]{:S(2)}) collective-permute-start(f32[1040,1,128]{2,0,1:T(8,128)S(1)} %get-tuple-element.78), channel_id=1, source_target_pairs={{1,0},{2,1},{3,2},{4,3},{5,4},{6,5},{7,6},{9,8},{10,9},{11,10},{12... | collective-permute-start | bytes 1597448 | tf_op jit(solution)/shard_map/ppermute | solution.py:29
  753.7 12.3 %collective-permute-start.42 = (f32[1040,1,128]{2,0,1:T(8,128)S(1)}, f32[1040,1,128]{2,0,1:T(8,128)S(1)}, u32[]{:S(2)}, u32[]{:S(2)}) collective-permute-start(f32[1040,1,128]{2,0,1:T(8,128)S(1)} %get-tuple-element.89), channel_id=1, source_target_pairs={{0,1},{1,2},{2,3},{3,4},{4,5},{5,6},{6,7},{8,9},{9,10},{10,11},{11... | collective-permute-start | bytes 1597448 | tf_op jit(solution)/shard_map/ppermute | solution.py:27
  755.3 22.2 %collective-permute-start.43 = (f32[1040,1,128]{2,0,1:T(8,128)S(1)}, f32[1040,1,128]{2,0,1:T(8,128)S(1)}, u32[]{:S(2)}, u32[]{:S(2)}) collective-permute-start(f32[1040,1,128]{2,0,1:T(8,128)S(1)} %get-tuple-element.90), channel_id=1, source_target_pairs={{1,0},{2,1},{3,2},{4,3},{5,4},{6,5},{7,6},{9,8},{10,9},{11,10},{12... | collective-permute-start | bytes 1597448 | tf_op jit(solution)/shard_map/ppermute | solution.py:29
  778.0 12.6 %collective-permute-start.44 = (f32[1040,1,128]{2,0,1:T(8,128)S(1)}, f32[1040,1,128]{2,0,1:T(8,128)S(1)}, u32[]{:S(2)}, u32[]{:S(2)}) collective-permute-start(f32[1040,1,128]{2,0,1:T(8,128)S(1)} %get-tuple-element.87), channel_id=1, source_target_pairs={{0,1},{1,2},{2,3},{3,4},{4,5},{5,6},{6,7},{8,9},{9,10},{10,11},{11... | collective-permute-start | bytes 1597448 | tf_op jit(solution)/shard_map/ppermute | solution.py:27
  779.5 23.8 %collective-permute-start.45 = (f32[1040,1,128]{2,0,1:T(8,128)S(1)}, f32[1040,1,128]{2,0,1:T(8,128)S(1)}, u32[]{:S(2)}, u32[]{:S(2)}) collective-permute-start(f32[1040,1,128]{2,0,1:T(8,128)S(1)} %get-tuple-element.88), channel_id=1, source_target_pairs={{1,0},{2,1},{3,2},{4,3},{5,4},{6,5},{7,6},{9,8},{10,9},{11,10},{12... | collective-permute-start | bytes 1597448 | tf_op jit(solution)/shard_map/ppermute | solution.py:29
  803.8 12.8 %collective-permute-start.46 = (f32[1040,1,128]{2,0,1:T(8,128)S(1)}, f32[1040,1,128]{2,0,1:T(8,128)S(1)}, u32[]{:S(2)}, u32[]{:S(2)}) collective-permute-start(f32[1040,1,128]{2,0,1:T(8,128)S(1)} %get-tuple-element.85), channel_id=1, source_target_pairs={{0,1},{1,2},{2,3},{3,4},{4,5},{5,6},{6,7},{8,9},{9,10},{10,11},{11... | collective-permute-start | bytes 1597448 | tf_op jit(solution)/shard_map/ppermute | solution.py:27
  805.6 23.5 %collective-permute-start.47 = (f32[1040,1,128]{2,0,1:T(8,128)S(1)}, f32[1040,1,128]{2,0,1:T(8,128)S(1)}, u32[]{:S(2)}, u32[]{:S(2)}) collective-permute-start(f32[1040,1,128]{2,0,1:T(8,128)S(1)} %get-tuple-element.86), channel_id=1, source_target_pairs={{1,0},{2,1},{3,2},{4,3},{5,4},{6,5},{7,6},{9,8},{10,9},{11,10},{12... | collective-permute-start | bytes 1597448 | tf_op jit(solution)/shard_map/ppermute | solution.py:29
  (89 other events, 1422.0 us)
where the time goes:
time: 845 us; the launch traced here: 834 us
  waiting for transfers between devices  333 us (39%)
  other arithmetic  202 us (24%)
  local copies, waits for them, and re-layouts  146 us (17%)
  starting transfers between devices  144 us (17%)
    ppermute x20, waiting for transfers between devices, with_halo(): lax.ppermute(head, axis, [((i + 1) % count, i) for i in range(ends)])  180 us
    ppermute x20, waiting for transfers between devices, with_halo(): lax.ppermute(tail, axis, [(i, (i + 1) % count) for i in range(ends)])  124 us
    scatter-add x8, other arithmetic, per_device(): adjoint.at[:, base_index + offsets[corner]]  95.8 us
    gather x16, local copies, waits for them, and re-layouts, per_device(): extended[:, base_index + offsets[corner]]  64 us
    ppermute x20, starting transfers between devices, with_halo(): lax.ppermute(tail, axis, [(i, (i + 1) % count) for i in range(ends)])  60.7 us
    select_n x16, other arithmetic, relax(): jnp.where(inside, grid_field + diffusion * (lower + upper - 2.0 * grid_fi...  38.5 us
    ppermute x8, starting transfers between devices, from_behind(): return lax.ppermute(block, axis, route)  35 us
    ppermute x20, starting transfers between devices, with_halo(): lax.ppermute(head, axis, [((i + 1) % count, i) for i in range(ends)])  30.6 us
  transfers between devices with their start and end apart: 50, of which 43 were waited for; matrix products, arithmetic and copies ran while one was open for 7% of the time, Pallas kernels for 0%

commit v1 on v0

v1 whole, which is shorter than its diff:
```python
import math

import jax
import jax.numpy as jnp
from jax import lax
from jax.experimental import pallas as pl
from jax.experimental.pallas import tpu as pltpu
from jax.sharding import PartitionSpec as P

f32, bf16, i32 = jnp.float32, jnp.bfloat16, jnp.int32
MESH = pl.DeviceIdType.MESH

MEMBERS = 128
ITERS = 2
ENS = 0.8660254037844386 / math.sqrt(MEMBERS - 1)
STATIC = 0.5
DESCENT = 0.2
GAIN = 4.0


def four_passes():
    taps = [1.0]
    for _ in range(4):
        wide = [0.0] * (len(taps) + 2)
        for i, t in enumerate(taps):
            wide[i] += 0.45 * t
            wide[i + 1] += 0.1 * t
            wide[i + 2] += 0.45 * t
        taps = wide
    return taps[4:]


TAP = four_passes()

CHUNK = 256
CHUNKS = 16
BELOW, ABOVE, OWN = 0, 1, 2


def split2(x):
    hi = x.astype(bf16)
    return hi, (x - hi.astype(f32)).astype(bf16)


def split3(x):
    hi = x.astype(bf16)
    rest = x - hi.astype(f32)
    mid = rest.astype(bf16)
    return hi, mid, (rest - mid.astype(f32)).astype(bf16)


def dot(a, b):
    return jnp.dot(a, b, preferred_element_type=f32)


def dot_nt(a, b):
    return lax.dot_general(a, b, (((1,), (1,)), ((), ())), preferred_element_type=f32)


def iota(shape, dim):
    return lax.broadcasted_iota(i32, shape, dim)


def tap_of(distance):
    out = jnp.zeros(distance.shape, f32)
    for d in range(5):
        out = jnp.where(distance == d, TAP[d], out)
    return out


def body(
    alpha, pert, stat, sig, coef, interp, oval, owgt, tile, cell,
    alpha_out, stat_out, inc_out,
    buf, xb, pack, side, wf, wa, y_s, yh_s, vh_s, eb, eh_s, msend, mrecv,
    f_dn, f_up, f_up2, f_mem, nsend, nrecv, gb, g_dn, g_up, g_dn2, gx_s, gh_s,
    feat, key_s, sb, tb, rb, qt, cm, ov, lh, gacc,
    ps, pr, fs, fr, as_, ar, o1s, o1r, o2s, o2r, ms, mr, bs, br, ns, nr, ds_, dr,
):
    mem, gx, gy = lax.axis_index("mem"), lax.axis_index("gx"), lax.axis_index("gy")
    ngx, ngy = lax.axis_size("gx"), lax.axis_size("gy")
    par = lax.rem(gy, 2)
    partner = gy + 1 - 2 * par
    gy_f = gy + 2 - 4 * par
    has_f = (gy_f >= 0) & (gy_f < ngy)
    gy_b = gy - 2 + 4 * par
    has_b = (gy_b >= 0) & (gy_b < ngy)
    top = jnp.where(gy == 0, 1.0, 0.0)
    bottom = jnp.where(gy == ngy - 1, 1.0, 0.0)
    west = jnp.where(gx == 0, 1.0, 0.0)
    east = jnp.where(gx == ngx - 1, 1.0, 0.0)
    has_l, has_r = gx > 0, gx < ngx - 1
    lane8 = iota((8, 128), 1)

    barrier = pltpu.get_barrier_semaphore()
    for j in range(1, ngx):
        pl.semaphore_signal(barrier, inc=1, device_id=(mem, lax.rem(gx + j, ngx), gy), device_id_type=MESH)
    for j in range(1, ngy):
        pl.semaphore_signal(barrier, inc=1, device_id=(mem, gx, lax.rem(gy + j, ngy)), device_id_type=MESH)
    for j in range(ngy):
        pl.semaphore_signal(barrier, inc=1, device_id=(1 - mem, gx, lax.rem(gy + j, ngy)), device_id_type=MESH)
    pl.semaphore_wait(barrier, ngx + 2 * ngy - 2)

    def remote(src, dst, s, r, device):
        return pltpu.make_async_remote_copy(
            src_ref=src, dst_ref=dst, send_sem=s, recv_sem=r, device_id=device, device_id_type=MESH
        )

    def rows_of(i):
        return pl.ds(pl.multiple_of(i * CHUNK, CHUNK), CHUNK)

    def direct(i):
        return remote(pert.at[rows_of(i)], buf.at[par, rows_of(i)], ps.at[i], pr.at[i], (mem, gx, partner))

    def arrival(i):
        return remote(pert.at[rows_of(i)], buf.at[1 - par, rows_of(i)], ps.at[i], pr.at[i], (mem, gx, partner))

    def forward(i):
        return remote(
            buf.at[1 - par, rows_of(i)], buf.at[par, rows_of(i)], fs.at[i], fr.at[i],
            (mem, gx, lax.rem(gy_f + ngy, ngy)),
        )

    def direct_x():
        return remote(xb.at[OWN], xb.at[par], ps.at[CHUNKS], pr.at[CHUNKS], (mem, gx, partner))

    def arrival_x():
        return remote(xb.at[OWN], xb.at[1 - par], ps.at[CHUNKS], pr.at[CHUNKS], (mem, gx, partner))

    def forward_x():
        return remote(
            xb.at[1 - par], xb.at[par], fs.at[CHUNKS], fr.at[CHUNKS], (mem, gx, lax.rem(gy_f + ngy, ngy))
        )

    def pump(i):
        arrival(i).wait_recv()

        @pl.when(has_f)
        def _():
            forward(i).start()

    def landed(i):
        @pl.when(has_b)
        def _():
            forward(i).wait_recv()

    for i in range(CHUNKS // 2):
        direct(i).start()

    @pl.when(jnp.logical_not(has_b))
    def _():
        @pl.loop(0, CHUNKS)
        def _(i):
            buf[par, rows_of(i), :] = jnp.zeros((CHUNK, 128), f32)

        xb[par] = jnp.zeros(xb.shape[1:], f32)

    @pl.when(gx == 0)
    def _():
        side[0] = jnp.zeros(side.shape[1:], f32)
        for it in range(ITERS):
            mrecv[it, 0] = jnp.zeros(mrecv.shape[2:], f32)
            nrecv[it, 0] = jnp.zeros(nrecv.shape[2:], f32)

    @pl.when(gx == ngx - 1)
    def _():
        side[1] = jnp.zeros(side.shape[1:], f32)
        for it in range(ITERS):
            mrecv[it, 1] = jnp.zeros(mrecv.shape[2:], f32)
            nrecv[it, 1] = jnp.zeros(nrecv.shape[2:], f32)

    @pl.when(gy == 0)
    def _():
        f_dn[...] = jnp.zeros(f_dn.shape, f32)
        g_dn[...] = jnp.zeros(g_dn.shape, f32)

    @pl.when(gy < 2)
    def _():
        g_dn2[...] = jnp.zeros(g_dn2.shape, f32)

    @pl.when(gy == ngy - 1)
    def _():
        f_up[...] = jnp.zeros(f_up.shape, f32)
        g_up[...] = jnp.zeros(g_up.shape, f32)

    @pl.when(gy >= ngy - 2)
    def _():
        f_up2[...] = jnp.zeros(f_up2.shape, f32)

    pack[...] = jnp.zeros(pack.shape, f32)
    px, pa = iota((128, 128), 0), iota((128, 128), 1)

    def selection(i):
        j = pa - 8 * i
        last = jnp.where((j >= 0) & (j < 4) & (px == 124 + j), 1.0, 0.0)
        first = jnp.where((j >= 4) & (j < 8) & (px == j - 4), 1.0, 0.0)
        return jnp.concatenate([last, first], axis=1).astype(bf16)

    @pl.loop(0, CHUNKS)
    def _(i):
        picked = dot(pert[rows_of(i), :].astype(bf16), selection(i))
        pack[0, :CHUNK] += picked[:, :128]
        pack[1, :CHUNK] += picked[:, 128:]

    scaled = sig[...] * (STATIC / ENS)
    xb[OWN, 320:384] = scaled
    hi, mid, lo = split3(scaled)
    sel = selection(0)
    picked = dot(hi, sel) + dot(mid, sel) + dot(lo, sel)
    pack[0, CHUNK:] = picked[:, :128]
    pack[1, CHUNK:] = picked[:, 128:]

    right, left = lax.rem(gx + 1, ngx), lax.rem(gx + ngx - 1, ngx)

    def to_right(src, dst, sems, recvs):
        return remote(src, dst, sems.at[0], recvs.at[0], (mem, right, gy))

    def to_left(src, dst, sems, recvs):
        return remote(src, dst, sems.at[1], recvs.at[1], (mem, left, gy))

    def exchange_lon(a_src, b_src, dst, sems, recvs):
        a, b = to_right(a_src, dst.at[0], sems, recvs), to_left(b_src, dst.at[1], sems, recvs)

        @pl.when(has_r)
        def _():
            a.start()

        @pl.when(has_l)
        def _():
            b.start()

        @pl.when(has_l)
        def _():
            a.wait_recv()

        @pl.when(has_r)
        def _():
            b.wait_recv()

        @pl.when(has_r)
        def _():
            a.wait_send()

        @pl.when(has_l)
        def _():
            b.wait_send()

    exchange_lon(pack.at[0], pack.at[1], side, as_, ar)
    xb[OWN, :320] = side[0] + side[1]
    direct_x().start()
    for i in range(CHUNKS // 2, CHUNKS):
        direct(i).start()
    pump(0)

    main = tap_of(jnp.abs(px - pa)) - west * tap_of(px + pa + 2) - east * tap_of(256 - px - pa)
    main_hi, main_lo = split2(main)

    @pl.loop(0, CHUNKS)
    def _(i):
        j = pa - 8 * i
        d = jnp.where(j < 4, px + 4 - j, 124 + j - px)
        h_hi, h_lo = split2(jnp.where((j >= 0) & (j < 8), tap_of(d), 0.0))
        wf[i, 0] = jnp.concatenate([main_hi, h_hi], axis=1)
        wf[i, 1] = jnp.concatenate([main_lo, h_lo], axis=1)
        j = px - 8 * i
        d = jnp.where(j < 4, pa + 4 - j, 124 + j - pa)
        h_hi, h_lo = split2(jnp.where((j >= 0) & (j < 8), tap_of(d), 0.0))
        wa[i, 0] = jnp.concatenate([main_hi, h_hi], axis=0)
        wa[i, 1] = jnp.concatenate([main_lo, h_lo], axis=0)

    pump(1)
    pump(2)

    tri = jnp.where(px < pa, 1.0, 0.0).astype(bf16)
    totals = jnp.zeros((64, 1), f32)
    for b in range(8):
        t = tile[:, b * 128 : (b + 1) * 128]
        one = jnp.where(iota((64, 128), 0) == t, 1.0, 0.0)
        before = dot(one.astype(bf16), tri) + totals
        rank = jnp.sum(before * one, axis=0, keepdims=True).astype(i32)
        totals = totals + jnp.sum(one, axis=1, keepdims=True)
        key_s[0:1, b * 128 : (b + 1) * 128] = (rank >> 3) * 512 + t * 8 + (rank & 7)
    feat[...] = jnp.zeros(feat.shape, f32)
    feat[0:16] = coef[...]
    feat[16:20] = interp[...]
    feat[20:21] = (cell[...] >> 9).astype(f32)
    feat[21:22] = ((cell[...] & 255) >> 1).astype(f32)
    feat[22:23] = oval[...]
    feat[23:24] = owgt[...]
    zero32 = jnp.zeros((32, 1024), bf16)

    @pl.loop(0, 4)
    def _(q):
        total = jnp.zeros((128, 128), f32)
        key = key_s[0:1, :]
        parts = split3(feat[...])
        for g in range(4):
            pick = jnp.where(iota((128, 1024), 0) + (g * 512 + q * 128) == key, 1.0, 0.0).astype(bf16)
            for part in parts:
                placed = jnp.concatenate([part if n == g else zero32 for n in range(4)], axis=0)
                total = total + dot_nt(pick, placed)
        sb[pl.ds(pl.multiple_of(q * 128, 128), 128), :] = total

    pump(3)
    pump(4)

    def o1(j):
        to = lax.rem(gx + j, ngx)
        return remote(
            sb.at[pl.ds(pl.multiple_of(to * 64, 64), 64)], tb.at[gx], o1s.at[j], o1r.at[gx], (mem, to, gy)
        )

    def o1_in(j):
        of = lax.rem(gx - j + ngx, ngx)
        return remote(sb.at[pl.ds(0, 64)], tb.at[of], o1s.at[j], o1r.at[of], (mem, of, gy))

    for j in range(1, ngx):
        o1(j).start()
    tb[gx] = sb[pl.ds(pl.multiple_of(gx * 64, 64), 64), :]
    for j in range(1, ngx):
        o1_in(j).wait_recv()

    def near(j):
        return mem if j % 2 == 0 else 1 - mem

    def o2(j):
        to = lax.rem(gy + j, ngy)
        return remote(
            tb.at[:, pl.ds(pl.multiple_of(to * 8, 8), 8)], rb.at[gy], o2s.at[j], o2r.at[gy], (near(j), gx, to)
        )

    def o2_in(j):
        of = lax.rem(gy - j + ngy, ngy)
        return remote(tb.at[:, pl.ds(0, 8)], rb.at[of], o2s.at[j], o2r.at[of], (near(j), gx, of))

    for j in range(1, ngy):
        o2(j).start()
    rb[gy] = tb[:, pl.ds(pl.multiple_of(gy * 8, 8), 8), :]
    pump(5)
    pump(6)
    for j in range(1, ngy):
        o2_in(j).wait_recv()

    @pl.loop(0, 4)
    def _(q):
        turned = rb[pl.ds(q * 2, 2)].reshape(128, 128).T
        for g in range(4):
            at = pl.ds(pl.multiple_of((g * 4 + q) * 128, 128), 128)
            f = turned[g * 32 : (g + 1) * 32]
            rr, xx = f[20:21], f[21:22]
            for dc in range(2):
                upper, lower = f[16 + dc : 17 + dc], f[18 + dc : 19 + dc]
                for row in range(5):
                    w = jnp.where(rr == float(row), upper, 0.0) + jnp.where(rr == float(row - 1), lower, 0.0)
                    qt[dc * 80 + row * 16 : dc * 80 + row * 16 + 16, at] = f[0:16] * w
            cm[:, at] = jnp.where(px.astype(f32) == xx, 1.0, 0.0).astype(bf16)
            ov[0:1, at] = f[22:23]
            ov[1:2, at] = f[23:24]

    pump(7)

    def lat(row, i):
        d = abs(row - i)
        if d > 4:
            return None
        c = GAIN * TAP[d]
        if 0 <= row < 4:
            if row + i + 2 <= 4:
                c = c - top * (GAIN * TAP[row + i + 2])
            if 8 - row - i <= 4:
                c = c - bottom * (GAIN * TAP[8 - row - i])
        return c

    COEF = [[lat(row - 4, i) for i in range(4)] for row in range(12)]

    def lat_out(y):
        z = []
        for row in range(12):
            acc = None
            for i in range(4):
                if COEF[row][i] is not None:
                    term = COEF[row][i] * y[i]
                    acc = term if acc is None else acc + term
            z.append(acc)
        return z

    def lat_in(q):
        v = []
        for i in range(4):
            acc = None
            for row in range(12):
                if COEF[row][i] is not None:
                    term = COEF[row][i] * q[row]
                    acc = term if acc is None else acc + term
            v.append(acc)
        return v

    def every4(start):
        return pl.ds(start, 8, stride=4)

    def pert_rows(start):
        at = [every4(start + r) for r in range(4)]
        return (
            [buf[BELOW, a, :] for a in at] + [pert[a, :] for a in at] + [buf[ABOVE, a, :] for a in at]
        )

    def xb_rows(start):
        return [xb[b, every4(start + r), :] for b in (BELOW, OWN, ABOVE) for r in range(4)]

    def lon(x, w, i):
        hi, lo = split2(x)
        return dot(hi, w[i, 0]) + dot(lo, w[i, 0]) + dot(hi, w[i, 1])

    def eb_at(row, c8):
        return pl.ds((row + 1) * 16 + c8 * 8, 8)

    def accumulate(y, first, count, rows):
        for c8 in range(2):
            acc = [eb[eb_at(row, c8), :] for row in range(12)]
            for k in range(count):
                start = k * 64 + c8 * 32
                z = lat_out([y[every4(first + start + r), :] for r in range(4)])
                p = rows(start)
                acc = [acc[row] + z[row] * p[row] for row in range(12)]
            for row in range(12):
                eb[eb_at(row, c8), :] = acc[row]

    def clear():
        eb[...] = jnp.zeros(eb.shape, f32)
        yh_s[...] = jnp.zeros(yh_s.shape, f32)

    def member_chunk(src, i):
        wide = lon(src[rows_of(i), :], wf, i)
        y_s[:CHUNK] = wide[:, :128]
        yh_s[:CHUNK] += wide[:, 128:]
        accumulate(y_s, 0, 4, lambda start: pert_rows(pl.multiple_of(i * CHUNK, CHUNK) + start))

    def static_chunk(src):
        wide = lon(src[...] * jnp.where(mem == 0, 1.0, 0.0), wf, 0)
        y_s[CHUNK:] = wide[:, :128]
        yh_s[CHUNK:] = wide[:, 128:]
        accumulate(y_s, CHUNK, 1, lambda start: xb_rows(320 + start))

    lane192 = iota((192, 128), 1)
    lane16 = iota((16, 128), 1)

    def around(x):
        for s in (8, 16, 32, 64):
            x = x + pltpu.roll(x, s, 1)
        return x

    def reduce_and_observe(it):
        for c8 in range(2):
            acc = [jnp.zeros((8, 128), f32) for _ in range(12)]
            for k in range(5):
                start = k * 64 + c8 * 32
                z = lat_out([yh_s[every4(start + r), :] for r in range(4)])
                p = xb_rows(start)
                acc = [acc[row] + z[row] * p[row] for row in range(12)]
            for row in range(12):
                eh_s[row * 16 + c8 * 8 : row * 16 + c8 * 8 + 8] = acc[row]
        eh = around(eh_s[...])
        e = eb[16:208]
        msend[...] = jnp.where(
            lane192 < 8,
            pltpu.roll(eh, 124, 1),
            jnp.where(lane192 >= 120, pltpu.roll(eh, 4, 1), jnp.where(lane192 == 16, pltpu.roll(e, 16, 1), 0.0)),
        )
        exchange_lon(msend, msend, mrecv.at[it], ms.at[it], mr.at[it])
        m_l, m_r = mrecv[it, 0], mrecv[it, 1]
        eb[16:208] = e + jnp.where(lane192 < 4, m_l, 0.0) + jnp.where(lane192 >= 124, m_r, 0.0)
        beyond = pltpu.roll(m_r, 112, 1) + msend[...]
        xv = jnp.zeros((16, 128), f32)
        for row in range(12):
            b = beyond[row * 16 : row * 16 + 16]
            xv = xv + jnp.where(lane16 == row, pltpu.roll(b, row, 1) if row else b, 0.0)
        eb[0:16] = xv
        eb[208:224] = xv

        def sends():
            out = []
            n = 0
            for flip in range(2):
                m = mem if flip == 0 else 1 - mem
                out.append((gy < ngy - 1, remote(eb.at[pl.ds(144, 80)], f_dn.at[it, mem], bs.at[it, n], br.at[it, n], (m, gx, lax.rem(gy + 1, ngy)))))
                out.append((gy > 0, remote(eb.at[pl.ds(0, 96)], f_up.at[it, mem], bs.at[it, n + 1], br.at[it, n + 1], (m, gx, lax.rem(gy + ngy - 1, ngy)))))
                out.append((gy > 1, remote(eb.at[pl.ds(0, 32)], f_up2.at[it, mem], bs.at[it, n + 2], br.at[it, n + 2], (m, gx, lax.rem(gy + ngy - 2, ngy)))))
                n += 3
            out.append((None, remote(eb.at[pl.ds(80, 80)], f_mem.at[it, pl.ds(0, 80)], bs.at[it, 6], br.at[it, 6], (1 - mem, gx, gy))))
            out.append((None, remote(eb.at[pl.ds(208, 16)], f_mem.at[it, pl.ds(80, 16)], bs.at[it, 7], br.at[it, 7], (1 - mem, gx, gy))))
            return out

        def receives():
            out = []
            n = 0
            for flip in range(2):
                m = mem if flip == 0 else 1 - mem
                out.append((gy > 0, remote(eb.at[pl.ds(144, 80)], f_dn.at[it, m], bs.at[it, n], br.at[it, n], (mem, gx, gy))))
                out.append((gy < ngy - 1, remote(eb.at[pl.ds(0, 96)], f_up.at[it, m], bs.at[it, n + 1], br.at[it, n + 1], (mem, gx, gy))))
                out.append((gy < ngy - 2, remote(eb.at[pl.ds(0, 32)], f_up2.at[it, m], bs.at[it, n + 2], br.at[it, n + 2], (mem, gx, gy))))
                n += 3
            out.append((None, remote(eb.at[pl.ds(80, 80)], f_mem.at[it, pl.ds(0, 80)], bs.at[it, 6], br.at[it, 6], (mem, gx, gy))))
            out.append((None, remote(eb.at[pl.ds(208, 16)], f_mem.at[it, pl.ds(80, 16)], bs.at[it, 7], br.at[it, 7], (mem, gx, gy))))
            return out

        run(sends(), "start")
        run(receives(), "wait_recv")
        run(sends(), "wait_send")

        def block_sum(own, own_xv, m):
            rows = []
            for r in range(5):
                t = own(r) + f_up[it, m, (r + 1) * 16 : (r + 2) * 16]
                if r < 4:
                    t = t + f_dn[it, m, r * 16 : r * 16 + 16]
                else:
                    t = t + f_up2[it, m, 16:32]
                rows.append(t)
            x = own_xv + pltpu.roll(f_dn[it, m, 64:80], 124, 1) + pltpu.roll(f_up[it, m, 0:16], 4, 1)
            x = x + pltpu.roll(jnp.where(lane16 == 0, f_up2[it, m, 0:16], 0.0), 8, 1)
            return rows, x

        mine, x_mine = block_sum(lambda r: eb[80 + r * 16 : 96 + r * 16], eb[208:224], mem)
        theirs, x_theirs = block_sum(lambda r: f_mem[it, r * 16 : r * 16 + 16], f_mem[it, 80:96], 1 - mem)
        x = (x_mine + x_theirs) * ENS
        for r in range(5):
            dx = (mine[r] + theirs[r]) * ENS
            moved = jnp.where(lane16 == 127, pltpu.roll(x, 127 - (r + 4), 1), pltpu.roll(dx, 127, 1))
            if it == ITERS - 1 and r < 4:
                inc_out[every4(r), :] = dx[:8]
                inc_out[every4(32 + r), :] = dx[8:]
            for n, v in ((0, dx), (1, moved)):
                hi, lo = split2(v)
                lh[0, n * 80 + r * 16 : n * 80 + r * 16 + 16] = hi
                lh[1, n * 80 + r * 16 : n * 80 + r * 16 + 16] = lo

        gacc[...] = jnp.zeros(gacc.shape, f32)

        @pl.loop(0, 8)
        def _(n):
            at = pl.ds(pl.multiple_of(n * 256, 256), 256)
            c = cm[:, at]
            u = dot(lh[0], c) + dot(lh[1], c)
            q = qt[:, at]
            hx = jnp.sum(q * u, axis=0, keepdims=True)
            misfit = ov[1:2, at] * (hx - ov[0:1, at])
            hi, lo = split2(q * misfit)
            gacc[...] += dot_nt(hi, c) + dot_nt(lo, c)

        lane80 = iota((80, 128), 1)
        g0, g1 = gacc[0:80], gacc[80:160]
        g5 = g0 + jnp.where(lane80 == 0, 0.0, pltpu.roll(g1, 1, 1))
        nsend[...] = jnp.where(lane80 == 64, pltpu.roll(g1, 65, 1), g5)
        exchange_lon(nsend, nsend, nrecv.at[it], ns.at[it], nr.at[it])
        n_l, n_r = nrecv[it, 0], nrecv[it, 1]
        gb[16:96] = g5 + jnp.where(lane80 == 0, pltpu.roll(n_l, 64, 1), 0.0)
        halo = jnp.where(
            lane80 < 4,
            pltpu.roll(n_l, 4, 1),
            jnp.where(lane80 < 8, pltpu.roll(n_r, 4, 1) + jnp.where(lane80 == 4, pltpu.roll(g1, 5, 1), 0.0), 0.0),
        )
        ghv = halo[0:16]
        for r in range(1, 5):
            ghv = ghv + pltpu.roll(halo[r * 16 : r * 16 + 16], 8 * r, 1)
        gb[0:16] = ghv
        gb[96:112] = ghv

        def sends_g():
            return [
                (gy < ngy - 1, remote(gb.at[pl.ds(16, 96)], g_dn.at[it], ds_.at[it, 0], dr.at[it, 0], (1 - mem, gx, lax.rem(gy + 1, ngy)))),
                (gy > 0, remote(gb.at[pl.ds(0, 80)], g_up.at[it], ds_.at[it, 1], dr.at[it, 1], (1 - mem, gx, lax.rem(gy + ngy - 1, ngy)))),
                (gy < ngy - 2, remote(gb.at[pl.ds(80, 32)], g_dn2.at[it], ds_.at[it, 2], dr.at[it, 2], (mem, gx, lax.rem(gy + 2, ngy)))),
            ]

        def receives_g():
            both = sends_g()
            return [(gy > 0, both[0][1]), (gy < ngy - 1, both[1][1]), (gy > 1, both[2][1])]

        run(sends_g(), "start")
        run(receives_g(), "wait_recv")
        run(sends_g(), "wait_send")

        def ext(v, r):
            return jnp.where(lane16 < 8, pltpu.roll(v, 128 - 8 * r, 1) if r else v, 0.0)

        for r in range(4):
            below, own, above = g_dn[it, r * 16 : r * 16 + 16], gb[16 + r * 16 : 32 + r * 16], g_up[it, 16 + r * 16 : 32 + r * 16]
            hb, ho, ha = ext(g_dn[it, 80:96], r), ext(ghv, r), ext(g_up[it, 0:16], r)
            if r == 0:
                below, hb = below + g_dn2[it, 0:16], hb + ext(g_dn2[it, 16:32], 4)
                own, ho = own + g_dn[it, 64:80], ho + ext(g_dn[it, 80:96], 4)
                above, ha = above + gb[80:96], ha + ext(ghv, 4)
            for n, (v, h) in enumerate(((below, hb), (own, ho), (above, ha))):
                at = n * 64 + r * 16
                gx_s[at : at + 16] = v
                gh_s[at : at + 16] = h
        gh_s[...] = around(gh_s[...])

        for c8 in range(2):
            g = [gh_s[row * 16 + c8 * 8 : row * 16 + c8 * 8 + 8] for row in range(12)]
            for k in range(5):
                start = k * 64 + c8 * 32
                p = xb_rows(start)
                v = lat_in([p[row] * g[row] for row in range(12)])
                for r in range(4):
                    yh_s[every4(start + r), :] = v[r]
        hi, lo = split2(yh_s[...])
        vh_s[0] = hi
        vh_s[1] = lo

    def run(copies, what):
        for condition, copy in copies:
            if condition is None:
                getattr(copy, what)()
            else:
                pl.when(condition)(lambda copy=copy: getattr(copy, what)())

    def gradient(first, count, halo, rows, i):
        for c8 in range(2):
            g = [gx_s[row * 16 + c8 * 8 : row * 16 + c8 * 8 + 8] for row in range(12)]
            for k in range(count):
                start = k * 64 + c8 * 32
                p = rows(start)
                v = lat_in([p[row] * g[row] for row in range(12)])
                for r in range(4):
                    y_s[every4(first + start + r), :] = v[r]
        n = count * 64
        hi, lo = split2(y_s[first : first + n])
        hi = jnp.concatenate([hi, vh_s[0, halo : halo + n]], axis=1)
        lo = jnp.concatenate([lo, vh_s[1, halo : halo + n]], axis=1)
        return dot(hi, wa[i, 0]) + dot(lo, wa[i, 0]) + dot(hi, wa[i, 1])

    def member_step(src, i):
        u = gradient(0, 4, 0, lambda start: pert_rows(pl.multiple_of(i * CHUNK, CHUNK) + start), i)
        alpha_out[rows_of(i), :] = (1.0 - DESCENT) * src[rows_of(i), :] - (DESCENT * ENS) * u

    def static_step(src):
        u = gradient(CHUNK, 1, CHUNK, lambda start: xb_rows(320 + start), 0)
        stat_out[...] = (1.0 - DESCENT) * src[...] - (DESCENT * ENS) * u

    clear()

    @pl.loop(0, CHUNKS // 2)
    def _(i):
        pump(i + CHUNKS // 2)
        landed(i)
        member_chunk(alpha, i)

    arrival_x().wait_recv()

    @pl.when(has_f)
    def _():
        forward_x().start()

    @pl.loop(CHUNKS // 2, CHUNKS)
    def _(i):
        landed(i)
        member_chunk(alpha, i)

    @pl.when(has_b)
    def _():
        forward_x().wait_recv()

    static_chunk(stat)
    reduce_and_observe(0)
    clear()

    @pl.loop(0, CHUNKS)
    def _(i):
        member_step(alpha, i)
        member_chunk(alpha_out, i)

    static_step(stat)
    static_chunk(stat_out)
    reduce_and_observe(1)

    @pl.loop(0, CHUNKS)
    def _(i):
        member_step(alpha_out, i)

    static_step(stat_out)

    for i in range(CHUNKS):
        direct(i).wait_send()
    direct_x().wait_send()

    @pl.when(has_f)
    def _():
        for i in range(CHUNKS):
            forward(i).wait_send()
        forward_x().wait_send()

    for j in range(1, ngx):
        o1(j).wait_send()
    for j in range(1, ngy):
        o2(j).wait_send()


def per_device(
    alpha, static_control, perturbations, sigma, obs_coef, interp_weights, obs_values, obs_weights, obs_tile, obs_cell
):
    rows = alpha.size // 128
    vmem = pl.BlockSpec(memory_space=pltpu.VMEM)
    args = (
        alpha.reshape(rows, 128),
        perturbations.astype(f32).reshape(rows, 128),
        static_control.reshape(64, 128),
        sigma.reshape(64, 128),
        obs_coef.reshape(16, 1024),
        interp_weights,
        obs_values.reshape(1, 1024),
        obs_weights.reshape(1, 1024),
        obs_tile.reshape(1, 1024),
        obs_cell.reshape(1, 1024),
    )
    dma = pltpu.SemaphoreType.DMA
    V = pltpu.VMEM
    scratch = [
        V((2, rows, 128), f32),
        V((3, 384, 128), f32),
        V((2, 320, 128), f32),
        V((2, 320, 128), f32),
        V((CHUNKS, 2, 128, 256), bf16),
        V((CHUNKS, 2, 256, 128), bf16),
        V((320, 128), f32),
        V((320, 128), f32),
        V((2, 320, 128), bf16),
        V((224, 128), f32),
        V((192, 128), f32),
        V((192, 128), f32),
        V((ITERS, 2, 192, 128), f32),
        V((ITERS, 2, 80, 128), f32),
        V((ITERS, 2, 96, 128), f32),
        V((ITERS, 2, 32, 128), f32),
        V((ITERS, 96, 128), f32),
        V((80, 128), f32),
        V((ITERS, 2, 80, 128), f32),
        V((112, 128), f32),
        V((ITERS, 96, 128), f32),
        V((ITERS, 80, 128), f32),
        V((ITERS, 32, 128), f32),
        V((192, 128), f32),
        V((192, 128), f32),
        V((32, 1024), f32),
        V((8, 1024), i32),
        V((512, 128), f32),
        V((8, 64, 128), f32),
        V((8, 8, 8, 128), f32),
        V((160, 2048), f32),
        V((128, 2048), bf16),
        V((8, 2048), f32),
        V((2, 160, 128), bf16),
        V((160, 128), f32),
        dma((CHUNKS + 1,)), dma((CHUNKS + 1,)), dma((CHUNKS + 1,)), dma((CHUNKS + 1,)),
        dma((2,)), dma((2,)),
        dma((8,)), dma((8,)), dma((8,)), dma((8,)),
        dma((ITERS, 2)), dma((ITERS, 2)),
        dma((ITERS, 8)), dma((ITERS, 8)),
        dma((ITERS, 2)), dma((ITERS, 2)),
        dma((ITERS, 3)), dma((ITERS, 3)),
    ]
    outs = pl.pallas_call(
        body,
        out_shape=(
            jax.ShapeDtypeStruct((rows, 128), f32),
            jax.ShapeDtypeStruct((64, 128), f32),
            jax.ShapeDtypeStruct((64, 128), f32),
        ),
        in_specs=[vmem] * len(args),
        out_specs=(vmem,) * 3,
        scratch_shapes=scratch,
        name="assimilate",
        compiler_params=pltpu.CompilerParams(
            collective_id=0, has_side_effects=True, vmem_limit_bytes=56 << 20
        ),
    )(*args)
    return (
        outs[0].reshape(alpha.shape),
        outs[1].reshape(static_control.shape),
        outs[2].reshape(static_control.shape),
    )


def solution(mesh):
    placed = (
        P("mem", None, None, "gy", "gx"),
        P(None, None, "gy", "gx"),
        P("mem", None, None, "gy", "gx"),
        P(None, None, "gy", "gx"),
        P(None, None, ("gx", "gy")),
        P(None, ("gx", "gy")),
        P(("gx", "gy")),
        P(("gx", "gy")),
        P(("gx", "gy"), None),
        P(("gx", "gy")),
    )
    return jax.shard_map(
        per_device,
        mesh=mesh,
        in_specs=placed,
        out_specs=(
            P("mem", None, None, "gy", "gx"),
            P(None, None, "gy", "gx"),
            P(None, None, "gy", "gx"),
        ),
        check_vma=False,
    )
```

time: 845 us -> 166 us (0.20); the launches traced: 834 us -> 166 us
  waiting for transfers between devices: 333 us -> 0 us
  other arithmetic: 202 us -> 2.68 us
  Pallas kernels: 0 us -> 158 us
  starting transfers between devices: 144 us -> 0 us
  local copies, waits for them, and re-layouts: 146 us -> 4.47 us
    ppermute x48 -> x0, waiting for transfers between devices: 320 us -> none  [the longest x20 180 us: with_halo(): lax.ppermute(head, axis, [((i + 1) % count, i) for i in range(ends)])]
    pallas_call x0 -> x1, Pallas kernels: none -> 158 us  [per_device(): pl.pallas_call(body, out_shape=(jax.ShapeDtypeStruct((rows, 128), f32), j...]
    ppermute x48 -> x0, starting transfers between devices: 126 us -> none  [the longest x20 60.7 us: with_halo(): lax.ppermute(tail, axis, [(i, (i + 1) % count) for i in range(ends)])]
    scatter-add x10 -> x0, other arithmetic: 95.8 us -> none  [the longest x8 95.8 us: per_device(): adjoint.at[:, base_index + offsets[corner]]]
    gather x16 -> x0, local copies, waits for them, and re-layouts: 64 us -> none  [per_device(): extended[:, base_index + offsets[corner]]]
    select_n x19 -> x0, other arithmetic: 38.6 us -> none  [the longest x16 38.5 us: relax(): jnp.where(inside, grid_field + diffusion * (lower + upper - 2.0 * grid_fi...]
    slice x42 -> x0, local copies, waits for them, and re-layouts: 30.1 us -> none  [the longest x20 12.5 us: with_halo(): lax.slice_in_dim(cells, cells.shape[dim] - width, cells.shape[dim], axis=...]
    concatenate x12 -> x0, other arithmetic: 27.3 us -> none  [the longest x4 16.4 us: with_halo(): jnp.concatenate([lax.ppermute(tail, axis, [(i, (i + 1) % count) for i in...]
  transfers between devices with their start and end apart: 50 -> 0, of which waited for: 43 -> 0; matrix products, arithmetic and copies ran while one was open for 7% -> 0% of each run, Pallas kernels for 0% -> 0%
where the time goes in v1:
time: 166 us
  Pallas kernels  158 us (95%)
  local copies, waits for them, and re-layouts  4.47 us (3%)
  other arithmetic  2.68 us (2%)
    pallas_call x1, Pallas kernels, per_device(): pl.pallas_call(body, out_shape=(jax.ShapeDtypeStruct((rows, 128), f32), j...  158 us
    unnamed x7, local copies, waits for them, and re-layouts  4.47 us

profile of v1, /device:TPU:1, one launch (start us, length us, event | category | flops | bytes accessed | tf_op | source)
XLA Modules:
  0.0 166.2 jit_solution(14540043823720180188)
XLA Ops:
  0.6 2.7 %convert.1.pert = f32[4096,128]{1,0:T(8,128)} convert(bf16[4096,128]{1,0:T(8,128)(2,1)} %bitcast.15) | non-fusion elementwise | flops 524288 | bytes 3145728 | tf_op jit(solution)/shard_map/reshape | solution.py:705
  3.3 158.3 %assimilate.1 = (f32[4096,128]{1,0:T(8,128)}, f32[64,128]{1,0:T(8,128)}, f32[64,128]{1,0:T(8,128)}) custom-call(f32[4096,128]{1,0:T(8,128)} %bitcast.13, f32[4096,128]{1,0:T(8,128)} %convert.1.pert, f32[64,128]{1,0:T(8,128)} %bitcast.17, f32[64,128]{1,0:T(8,128)} %bitcast.18, f32[16,1024]{1,0:T(8,128)} %bitcast.16, f32[4,1024]{1,0:T(4,128)} %interp.1, ...), custom_call_target="tpu_custom_call" | custom-call | tf_op jit(solution)/shard_map/assimilate/pallas_call | solution.py:761
  161.7 0.0 copy-start.1
  161.7 0.0 copy-start
  161.7 3.2 %copy.16 = f32[64,2,8,4,128]{4,3,2,1,0:T(4,128)} copy(f32[64,2,8,4,128]{4,3,2,1,0:T(4,128)} %bitcast.14) | data formatting | bytes 4194304
  164.9 0.0 copy-done.1
  164.9 0.6 copy.17
  165.5 0.0 copy-done
  165.5 0.6 copy.18
Async XLA Ops:
  161.7 3.3 %copy-start.1 = (f32[64,128]{1,0:T(8,128)S(1)}, f32[64,128]{1,0:T(8,128)}, u32[]{:S(2)}) copy-start(f32[64,128]{1,0:T(8,128)} %get-tuple-element.7) | copy-start | bytes 98308
  161.7 3.9 %copy-start = (f32[64,128]{1,0:T(8,128)S(1)}, f32[64,128]{1,0:T(8,128)}, u32[]{:S(2)}) copy-start(f32[64,128]{1,0:T(8,128)} %get-tuple-element.8) | copy-start | bytes 98308

commit v2 on v1

--- a/solution.py
+++ b/solution.py
@@ -34,6 +34,7 @@
 
 CHUNK = 256
 CHUNKS = 16
+AHEAD = 5
 BELOW, ABOVE, OWN = 0, 1, 2
 
 
@@ -71,10 +72,10 @@
 def body(
     alpha, pert, stat, sig, coef, interp, oval, owgt, tile, cell,
     alpha_out, stat_out, inc_out,
-    buf, xb, pack, side, wf, wa, y_s, yh_s, vh_s, eb, eh_s, msend, mrecv,
+    own, work, buf, xb, pack, side, wf, wa, y_s, yh_s, vh_s, eb, eh_s, msend, mrecv,
     f_dn, f_up, f_up2, f_mem, nsend, nrecv, gb, g_dn, g_up, g_dn2, gx_s, gh_s,
-    feat, key_s, sb, tb, rb, qt, cm, ov, lh, gacc,
-    ps, pr, fs, fr, as_, ar, o1s, o1r, o2s, o2r, ms, mr, bs, br, ns, nr, ds_, dr,
+    feat, ft, key_s, sb, tb, rb, qt, cm, ov, lh, gacc,
+    ps, pr, fs, fr, as_, ar, o1s, o1r, o2s, o2r, ms, mr, bs, br, ns, nr, ds_, dr, al, ao,
 ):
     mem, gx, gy = lax.axis_index("mem"), lax.axis_index("gx"), lax.axis_index("gy")
     ngx, ngy = lax.axis_size("gx"), lax.axis_size("gy")
@@ -109,10 +110,10 @@
         return pl.ds(pl.multiple_of(i * CHUNK, CHUNK), CHUNK)
 
     def direct(i):
-        return remote(pert.at[rows_of(i)], buf.at[par, rows_of(i)], ps.at[i], pr.at[i], (mem, gx, partner))
+        return remote(own.at[rows_of(i)], buf.at[par, rows_of(i)], ps.at[i], pr.at[i], (mem, gx, partner))
 
     def arrival(i):
-        return remote(pert.at[rows_of(i)], buf.at[1 - par, rows_of(i)], ps.at[i], pr.at[i], (mem, gx, partner))
+        return remote(own.at[rows_of(i)], buf.at[1 - par, rows_of(i)], ps.at[i], pr.at[i], (mem, gx, partner))
 
     def forward(i):
         return remote(
@@ -131,20 +132,29 @@
             xb.at[1 - par], xb.at[par], fs.at[CHUNKS], fr.at[CHUNKS], (mem, gx, lax.rem(gy_f + ngy, ngy))
         )
 
+    def issue(i):
+        own[rows_of(i), :] = pert[rows_of(i), :].astype(f32)
+        direct(i).start()
+
     def pump(i):
         arrival(i).wait_recv()
 
         @pl.when(has_f)
         def _():
             forward(i).start()
+
+        if isinstance(i, int) and i + AHEAD < CHUNKS:
+            issue(i + AHEAD)
 
     def landed(i):
         @pl.when(has_b)
         def _():
             forward(i).wait_recv()
 
-    for i in range(CHUNKS // 2):
-        direct(i).start()
+    for i in range(AHEAD):
+        issue(i)
+    fetch = pltpu.make_async_copy(alpha, work, al.at[0])
+    fetch.start()
 
     @pl.when(jnp.logical_not(has_b))
     def _():
@@ -197,7 +207,7 @@
 
     @pl.loop(0, CHUNKS)
     def _(i):
-        picked = dot(pert[rows_of(i), :].astype(bf16), selection(i))
+        picked = dot(pert[rows_of(i), :], selection(i))
         pack[0, :CHUNK] += picked[:, :128]
         pack[1, :CHUNK] += picked[:, 128:]
 
@@ -217,7 +227,7 @@
     def to_left(src, dst, sems, recvs):
         return remote(src, dst, sems.at[1], recvs.at[1], (mem, left, gy))
 
-    def exchange_lon(a_src, b_src, dst, sems, recvs):
+    def exchange_lon(a_src, b_src, dst, sems, recvs, wait=True):
         a, b = to_right(a_src, dst.at[0], sems, recvs), to_left(b_src, dst.at[1], sems, recvs)
 
         @pl.when(has_r)
@@ -228,6 +238,10 @@
         def _():
             b.start()
 
+        if wait:
+            finish_lon(a, b)
+
+    def finish_lon(a, b):
         @pl.when(has_l)
         def _():
             a.wait_recv()
@@ -244,31 +258,8 @@
         def _():
             b.wait_send()
 
-    exchange_lon(pack.at[0], pack.at[1], side, as_, ar)
-    xb[OWN, :320] = side[0] + side[1]
-    direct_x().start()
-    for i in range(CHUNKS // 2, CHUNKS):
-        direct(i).start()
+    exchange_lon(pack.at[0], pack.at[1], side, as_, ar, False)
     pump(0)
-
-    main = tap_of(jnp.abs(px - pa)) - west * tap_of(px + pa + 2) - east * tap_of(256 - px - pa)
-    main_hi, main_lo = split2(main)
-
-    @pl.loop(0, CHUNKS)
-    def _(i):
-        j = pa - 8 * i
-        d = jnp.where(j < 4, px + 4 - j, 124 + j - px)
-        h_hi, h_lo = split2(jnp.where((j >= 0) & (j < 8), tap_of(d), 0.0))
-        wf[i, 0] = jnp.concatenate([main_hi, h_hi], axis=1)
-        wf[i, 1] = jnp.concatenate([main_lo, h_lo], axis=1)
-        j = px - 8 * i
-        d = jnp.where(j < 4, pa + 4 - j, 124 + j - pa)
-        h_hi, h_lo = split2(jnp.where((j >= 0) & (j < 8), tap_of(d), 0.0))
-        wa[i, 0] = jnp.concatenate([main_hi, h_hi], axis=0)
-        wa[i, 1] = jnp.concatenate([main_lo, h_lo], axis=0)
-
-    pump(1)
-    pump(2)
 
     tri = jnp.where(px < pa, 1.0, 0.0).astype(bf16)
     totals = jnp.zeros((64, 1), f32)
@@ -286,22 +277,29 @@
     feat[21:22] = ((cell[...] & 255) >> 1).astype(f32)
     feat[22:23] = oval[...]
     feat[23:24] = owgt[...]
-    zero32 = jnp.zeros((32, 1024), bf16)
-
-    @pl.loop(0, 4)
-    def _(q):
+    for n, part in enumerate(split3(feat[...])):
+        ft[n * 32 : (n + 1) * 32] = part
+    ft[96:128] = jnp.zeros((32, 1024), bf16)
+    pump(1)
+
+    def sort_records(q):
         total = jnp.zeros((128, 128), f32)
         key = key_s[0:1, :]
-        parts = split3(feat[...])
+        lane = iota((128, 128), 1)
         for g in range(4):
             pick = jnp.where(iota((128, 1024), 0) + (g * 512 + q * 128) == key, 1.0, 0.0).astype(bf16)
-            for part in parts:
-                placed = jnp.concatenate([part if n == g else zero32 for n in range(4)], axis=0)
-                total = total + dot_nt(pick, placed)
-        sb[pl.ds(pl.multiple_of(q * 128, 128), 128), :] = total
-
+            x = dot_nt(pick, ft[...])
+            x = x + pltpu.roll(x, 96, 1) + pltpu.roll(x, 64, 1)
+            x = pltpu.roll(x, 32 * g, 1) if g else x
+            total = total + jnp.where((lane >= 32 * g) & (lane < 32 * g + 32), x, 0.0)
+        sb[q * 128 : (q + 1) * 128] = total
+
+    sort_records(0)
+    pump(2)
+    sort_records(1)
+    sort_records(2)
     pump(3)
-    pump(4)
+    sort_records(3)
 
     def o1(j):
         to = lax.rem(gx + j, ngx)
@@ -316,6 +314,30 @@
     for j in range(1, ngx):
         o1(j).start()
     tb[gx] = sb[pl.ds(pl.multiple_of(gx * 64, 64), 64), :]
+    finish_lon(to_right(pack.at[0], side.at[0], as_, ar), to_left(pack.at[1], side.at[1], as_, ar))
+    xb[OWN, :320] = side[0] + side[1]
+    direct_x().start()
+    pump(4)
+
+    main = tap_of(jnp.abs(px - pa)) - west * tap_of(px + pa + 2) - east * tap_of(256 - px - pa)
+    main_hi, main_lo = split2(main)
+
+    def matrices(first, last):
+        @pl.loop(first, last)
+        def _(i):
+            j = pa - 8 * i
+            d = jnp.where(j < 4, px + 4 - j, 124 + j - px)
+            h_hi, h_lo = split2(jnp.where((j >= 0) & (j < 8), tap_of(d), 0.0))
+            wf[i, 0] = jnp.concatenate([main_hi, h_hi], axis=1)
+            wf[i, 1] = jnp.concatenate([main_lo, h_lo], axis=1)
+            j = px - 8 * i
+            d = jnp.where(j < 4, pa + 4 - j, 124 + j - pa)
+            h_hi, h_lo = split2(jnp.where((j >= 0) & (j < 8), tap_of(d), 0.0))
+            wa[i, 0] = jnp.concatenate([main_hi, h_hi], axis=0)
+            wa[i, 1] = jnp.concatenate([main_lo, h_lo], axis=0)
+
+    matrices(0, 8)
+    pump(5)
     for j in range(1, ngx):
         o1_in(j).wait_recv()
 
@@ -335,16 +357,14 @@
     for j in range(1, ngy):
         o2(j).start()
     rb[gy] = tb[:, pl.ds(pl.multiple_of(gy * 8, 8), 8), :]
-    pump(5)
     pump(6)
-    for j in range(1, ngy):
-        o2_in(j).wait_recv()
-
-    @pl.loop(0, 4)
-    def _(q):
-        turned = rb[pl.ds(q * 2, 2)].reshape(128, 128).T
+    matrices(8, CHUNKS)
+    pump(7)
+
+    def operator(q):
+        turned = rb[q * 2 : q * 2 + 2].reshape(128, 128).T
         for g in range(4):
-            at = pl.ds(pl.multiple_of((g * 4 + q) * 128, 128), 128)
+            at = pl.ds((g * 4 + q) * 128, 128)
             f = turned[g * 32 : (g + 1) * 32]
             rr, xx = f[20:21], f[21:22]
             for dc in range(2):
@@ -355,8 +375,6 @@
             cm[:, at] = jnp.where(px.astype(f32) == xx, 1.0, 0.0).astype(bf16)
             ov[0:1, at] = f[22:23]
             ov[1:2, at] = f[23:24]
-
-    pump(7)
 
     def lat(row, i):
         d = abs(row - i)
@@ -400,7 +418,7 @@
     def pert_rows(start):
         at = [every4(start + r) for r in range(4)]
         return (
-            [buf[BELOW, a, :] for a in at] + [pert[a, :] for a in at] + [buf[ABOVE, a, :] for a in at]
+            [buf[BELOW, a, :] for a in at] + [own[a, :] for a in at] + [buf[ABOVE, a, :] for a in at]
         )
 
     def xb_rows(start):
@@ -629,9 +647,12 @@
         lo = jnp.concatenate([lo, vh_s[1, halo : halo + n]], axis=1)
         return dot(hi, wa[i, 0]) + dot(lo, wa[i, 0]) + dot(hi, wa[i, 1])
 
-    def member_step(src, i):
+    def member_step(i):
         u = gradient(0, 4, 0, lambda start: pert_rows(pl.multiple_of(i * CHUNK, CHUNK) + start), i)
-        alpha_out[rows_of(i), :] = (1.0 - DESCENT) * src[rows_of(i), :] - (DESCENT * ENS) * u
+        work[rows_of(i), :] = (1.0 - DESCENT) * work[rows_of(i), :] - (DESCENT * ENS) * u
+
+    def done(i):
+        return pltpu.make_async_copy(work.at[rows_of(i)], alpha_out.at[rows_of(i)], ao.at[i])
 
     def static_step(src):
         u = gradient(CHUNK, 1, CHUNK, lambda start: xb_rows(320 + start), 0)
@@ -639,11 +660,20 @@
 
     clear()
 
-    @pl.loop(0, CHUNKS // 2)
-    def _(i):
-        pump(i + CHUNKS // 2)
-        landed(i)
-        member_chunk(alpha, i)
+    fetch.wait()
+    for i in range(8, CHUNKS):
+        pump(i)
+        if i == 10:
+            for j in range(1, ngy):
+                o2_in(j).wait_recv()
+        if i >= 11 and i < 15:
+            operator(i - 11)
+        if i < 15:
+
+            @pl.loop(2 * (i - 8), 2 * (i - 8) + 2)
+            def _(n):
+                landed(n)
+                member_chunk(work, n)
 
     arrival_x().wait_recv()
 
@@ -651,10 +681,10 @@
     def _():
         forward_x().start()
 
-    @pl.loop(CHUNKS // 2, CHUNKS)
+    @pl.loop(CHUNKS - 2, CHUNKS)
     def _(i):
         landed(i)
-        member_chunk(alpha, i)
+        member_chunk(work, i)
 
     @pl.when(has_b)
     def _():
@@ -666,8 +696,8 @@
 
     @pl.loop(0, CHUNKS)
     def _(i):
-        member_step(alpha, i)
-        member_chunk(alpha_out, i)
+        member_step(i)
+        member_chunk(work, i)
 
     static_step(stat)
     static_chunk(stat_out)
@@ -675,9 +705,12 @@
 
     @pl.loop(0, CHUNKS)
     def _(i):
-        member_step(alpha_out, i)
+        member_step(i)
+        done(i).start()
 
     static_step(stat_out)
+    for i in range(CHUNKS):
+        done(i).wait()
 
     for i in range(CHUNKS):
         direct(i).wait_send()
@@ -702,7 +735,7 @@
     vmem = pl.BlockSpec(memory_space=pltpu.VMEM)
     args = (
         alpha.reshape(rows, 128),
-        perturbations.astype(f32).reshape(rows, 128),
+        perturbations.reshape(rows, 128),
         static_control.reshape(64, 128),
         sigma.reshape(64, 128),
         obs_coef.reshape(16, 1024),
@@ -715,6 +748,8 @@
     dma = pltpu.SemaphoreType.DMA
     V = pltpu.VMEM
     scratch = [
+        V((rows, 128), f32),
+        V((rows, 128), f32),
         V((2, rows, 128), f32),
         V((3, 384, 128), f32),
         V((2, 320, 128), f32),
@@ -741,6 +776,7 @@
         V((192, 128), f32),
         V((192, 128), f32),
         V((32, 1024), f32),
+        V((128, 1024), bf16),
         V((8, 1024), i32),
         V((512, 128), f32),
         V((8, 64, 128), f32),
@@ -757,6 +793,7 @@
         dma((ITERS, 8)), dma((ITERS, 8)),
         dma((ITERS, 2)), dma((ITERS, 2)),
         dma((ITERS, 3)), dma((ITERS, 3)),
+        dma((1,)), dma((CHUNKS,)),
     ]
     outs = pl.pallas_call(
         body,
@@ -765,8 +802,8 @@
             jax.ShapeDtypeStruct((64, 128), f32),
             jax.ShapeDtypeStruct((64, 128), f32),
         ),
-        in_specs=[vmem] * len(args),
-        out_specs=(vmem,) * 3,
+        in_specs=[pl.BlockSpec(memory_space=pl.ANY)] + [vmem] * (len(args) - 1),
+        out_specs=(pl.BlockSpec(memory_space=pl.ANY), vmem, vmem),
         scratch_shapes=scratch,
         name="assimilate",
         compiler_params=pltpu.CompilerParams(

time: 166 us -> 151 us (0.910)
  Pallas kernels: 158 us -> 146 us
  other arithmetic: 2.68 us -> 0 us
    pallas_call x1, Pallas kernels: 158 us -> 146 us  [per_device(): pl.pallas_call(body, out_shape=(jax.ShapeDtypeStruct((rows, 128), f32), j...]
    reshape x1 -> x0, other arithmetic: 2.68 us -> none  [per_device(): perturbations.astype(f32).reshape(rows, 128)]
where the time goes in v2:
time: 151 us
  Pallas kernels  146 us (97%)
  local copies, waits for them, and re-layouts  4.47 us (3%)
    pallas_call x1, Pallas kernels, per_device(): pl.pallas_call(body, out_shape=(jax.ShapeDtypeStruct((rows, 128), f32), j...  146 us
    unnamed x7, local copies, waits for them, and re-layouts  4.47 us

profile of v2, /device:TPU:1, one launch (start us, length us, event | category | flops | bytes accessed | tf_op | source)
XLA Modules:
  0.0 151.1 jit_solution(1603998393199165364)
XLA Ops:
  0.6 146.0 %assimilate.1 = (f32[4096,128]{1,0:T(8,128)}, f32[64,128]{1,0:T(8,128)}, f32[64,128]{1,0:T(8,128)}) custom-call(f32[4096,128]{1,0:T(8,128)} %bitcast.12, bf16[4096,128]{1,0:T(8,128)(2,1)} %bitcast.14, f32[64,128]{1,0:T(8,128)} %bitcast.16, f32[64,128]{1,0:T(8,128)} %bitcast.17, f32[16,1024]{1,0:T(8,128)} %bitcast.15, f32[4,1024]{1,0:T(4,128)} %interp.1, ...), custom_call_target="tpu_custom_call" | custom-call | tf_op jit(solution)/shard_map/assimilate/pallas_call | solution.py:798
  146.6 0.0 copy-start.1
  146.6 0.0 copy-start
  146.6 3.2 %copy.16 = f32[64,2,8,4,128]{4,3,2,1,0:T(4,128)} copy(f32[64,2,8,4,128]{4,3,2,1,0:T(4,128)} %bitcast.13) | data formatting | bytes 4194304
  149.9 0.0 copy-done.1
  149.9 0.6 copy.17
  150.5 0.0 copy-done
  150.5 0.6 copy.18
Async XLA Ops:
  146.6 3.3 %copy-start.1 = (f32[64,128]{1,0:T(8,128)S(1)}, f32[64,128]{1,0:T(8,128)}, u32[]{:S(2)}) copy-start(f32[64,128]{1,0:T(8,128)} %get-tuple-element.7) | copy-start | bytes 98308
  146.6 3.9 %copy-start = (f32[64,128]{1,0:T(8,128)S(1)}, f32[64,128]{1,0:T(8,128)}, u32[]{:S(2)}) copy-start(f32[64,128]{1,0:T(8,128)} %get-tuple-element.8) | copy-start | bytes 98308

commit v3 on v2

--- a/solution.py
+++ b/solution.py
@@ -34,7 +34,7 @@
 
 CHUNK = 256
 CHUNKS = 16
-AHEAD = 5
+AHEAD = 3
 BELOW, ABOVE, OWN = 0, 1, 2
 
 
@@ -73,7 +73,7 @@
     alpha, pert, stat, sig, coef, interp, oval, owgt, tile, cell,
     alpha_out, stat_out, inc_out,
     own, work, buf, xb, pack, side, wf, wa, y_s, yh_s, vh_s, eb, eh_s, msend, mrecv,
-    f_dn, f_up, f_up2, f_mem, nsend, nrecv, gb, g_dn, g_up, g_dn2, gx_s, gh_s,
+    f_dn, f_up, f_up2, f_mem, nrecv, gb, g_dn, g_up, g_dn2, gx_s, gh_s,
     feat, ft, key_s, sb, tb, rb, qt, cm, ov, lh, gacc,
     ps, pr, fs, fr, as_, ar, o1s, o1r, o2s, o2r, ms, mr, bs, br, ns, nr, ds_, dr, al, ao,
 ):
@@ -93,13 +93,23 @@
     lane8 = iota((8, 128), 1)
 
     barrier = pltpu.get_barrier_semaphore()
+
+    def greet(m, x, y):
+        pl.semaphore_signal(barrier, inc=1, device_id=(m, lax.rem(x + ngx, ngx), lax.rem(y + ngy, ngy)), device_id_type=MESH)
+
     for j in range(1, ngx):
-        pl.semaphore_signal(barrier, inc=1, device_id=(mem, lax.rem(gx + j, ngx), gy), device_id_type=MESH)
+        greet(mem, gx + j, gy)
     for j in range(1, ngy):
-        pl.semaphore_signal(barrier, inc=1, device_id=(mem, gx, lax.rem(gy + j, ngy)), device_id_type=MESH)
+        greet(mem, gx, gy + j)
     for j in range(ngy):
-        pl.semaphore_signal(barrier, inc=1, device_id=(1 - mem, gx, lax.rem(gy + j, ngy)), device_id_type=MESH)
-    pl.semaphore_wait(barrier, ngx + 2 * ngy - 2)
+        greet(1 - mem, gx, gy + j)
+    for dx in (-1, 1):
+        greet(1 - mem, gx + dx, gy)
+        for dy in (-1, 1):
+            greet(1 - mem, gx + dx, gy + dy)
+        for dy in (-2, 2):
+            greet(mem, gx + dx, gy + dy)
+    pl.semaphore_wait(barrier, ngx + 2 * ngy - 2 + 10)
 
     def remote(src, dst, s, r, device):
         return pltpu.make_async_remote_copy(
@@ -169,97 +179,42 @@
         side[0] = jnp.zeros(side.shape[1:], f32)
         for it in range(ITERS):
             mrecv[it, 0] = jnp.zeros(mrecv.shape[2:], f32)
-            nrecv[it, 0] = jnp.zeros(nrecv.shape[2:], f32)
+            for n in range(4):
+                nrecv[it, n, 0] = jnp.zeros((16, 128), f32)
 
     @pl.when(gx == ngx - 1)
     def _():
         side[1] = jnp.zeros(side.shape[1:], f32)
         for it in range(ITERS):
             mrecv[it, 1] = jnp.zeros(mrecv.shape[2:], f32)
-            nrecv[it, 1] = jnp.zeros(nrecv.shape[2:], f32)
+            for n in range(4):
+                nrecv[it, n, 1] = jnp.zeros((16, 128), f32)
 
     @pl.when(gy == 0)
     def _():
         f_dn[...] = jnp.zeros(f_dn.shape, f32)
         g_dn[...] = jnp.zeros(g_dn.shape, f32)
+        for it in range(ITERS):
+            nrecv[it, 1] = jnp.zeros((2, 16, 128), f32)
 
     @pl.when(gy < 2)
     def _():
         g_dn2[...] = jnp.zeros(g_dn2.shape, f32)
+        for it in range(ITERS):
+            nrecv[it, 3] = jnp.zeros((2, 16, 128), f32)
 
     @pl.when(gy == ngy - 1)
     def _():
         f_up[...] = jnp.zeros(f_up.shape, f32)
         g_up[...] = jnp.zeros(g_up.shape, f32)
+        for it in range(ITERS):
+            nrecv[it, 2] = jnp.zeros((2, 16, 128), f32)
 
     @pl.when(gy >= ngy - 2)
     def _():
         f_up2[...] = jnp.zeros(f_up2.shape, f32)
 
-    pack[...] = jnp.zeros(pack.shape, f32)
     px, pa = iota((128, 128), 0), iota((128, 128), 1)
-
-    def selection(i):
-        j = pa - 8 * i
-        last = jnp.where((j >= 0) & (j < 4) & (px == 124 + j), 1.0, 0.0)
-        first = jnp.where((j >= 4) & (j < 8) & (px == j - 4), 1.0, 0.0)
-        return jnp.concatenate([last, first], axis=1).astype(bf16)
-
-    @pl.loop(0, CHUNKS)
-    def _(i):
-        picked = dot(pert[rows_of(i), :], selection(i))
-        pack[0, :CHUNK] += picked[:, :128]
-        pack[1, :CHUNK] += picked[:, 128:]
-
-    scaled = sig[...] * (STATIC / ENS)
-    xb[OWN, 320:384] = scaled
-    hi, mid, lo = split3(scaled)
-    sel = selection(0)
-    picked = dot(hi, sel) + dot(mid, sel) + dot(lo, sel)
-    pack[0, CHUNK:] = picked[:, :128]
-    pack[1, CHUNK:] = picked[:, 128:]
-
-    right, left = lax.rem(gx + 1, ngx), lax.rem(gx + ngx - 1, ngx)
-
-    def to_right(src, dst, sems, recvs):
-        return remote(src, dst, sems.at[0], recvs.at[0], (mem, right, gy))
-
-    def to_left(src, dst, sems, recvs):
-        return remote(src, dst, sems.at[1], recvs.at[1], (mem, left, gy))
-
-    def exchange_lon(a_src, b_src, dst, sems, recvs, wait=True):
-        a, b = to_right(a_src, dst.at[0], sems, recvs), to_left(b_src, dst.at[1], sems, recvs)
-
-        @pl.when(has_r)
-        def _():
-            a.start()
-
-        @pl.when(has_l)
-        def _():
-            b.start()
-
-        if wait:
-            finish_lon(a, b)
-
-    def finish_lon(a, b):
-        @pl.when(has_l)
-        def _():
-            a.wait_recv()
-
-        @pl.when(has_r)
-        def _():
-            b.wait_recv()
-
-        @pl.when(has_r)
-        def _():
-            a.wait_send()
-
-        @pl.when(has_l)
-        def _():
-            b.wait_send()
-
-    exchange_lon(pack.at[0], pack.at[1], side, as_, ar, False)
-    pump(0)
 
     tri = jnp.where(px < pa, 1.0, 0.0).astype(bf16)
     totals = jnp.zeros((64, 1), f32)
@@ -280,7 +235,7 @@
     for n, part in enumerate(split3(feat[...])):
         ft[n * 32 : (n + 1) * 32] = part
     ft[96:128] = jnp.zeros((32, 1024), bf16)
-    pump(1)
+    pump(0)
 
     def sort_records(q):
         total = jnp.zeros((128, 128), f32)
@@ -295,11 +250,11 @@
         sb[q * 128 : (q + 1) * 128] = total
 
     sort_records(0)
+    sort_records(1)
+    pump(1)
+    sort_records(2)
+    sort_records(3)
     pump(2)
-    sort_records(1)
-    sort_records(2)
-    pump(3)
-    sort_records(3)
 
     def o1(j):
         to = lax.rem(gx + j, ngx)
@@ -314,9 +269,70 @@
     for j in range(1, ngx):
         o1(j).start()
     tb[gx] = sb[pl.ds(pl.multiple_of(gx * 64, 64), 64), :]
-    finish_lon(to_right(pack.at[0], side.at[0], as_, ar), to_left(pack.at[1], side.at[1], as_, ar))
-    xb[OWN, :320] = side[0] + side[1]
-    direct_x().start()
+    pump(3)
+
+    pack[...] = jnp.zeros(pack.shape, f32)
+
+    def selection(i):
+        j = pa - 8 * i
+        last = jnp.where((j >= 0) & (j < 4) & (px == 124 + j), 1.0, 0.0)
+        first = jnp.where((j >= 4) & (j < 8) & (px == j - 4), 1.0, 0.0)
+        return jnp.concatenate([last, first], axis=1).astype(bf16)
+
+    @pl.loop(0, CHUNKS)
+    def _(i):
+        picked = dot(pert[rows_of(i), :], selection(i))
+        pack[0, :CHUNK] += picked[:, :128]
+        pack[1, :CHUNK] += picked[:, 128:]
+
+    scaled = sig[...] * (STATIC / ENS)
+    xb[OWN, 320:384] = scaled
+    hi, mid, lo = split3(scaled)
+    sel = selection(0)
+    picked = dot(hi, sel) + dot(mid, sel) + dot(lo, sel)
+    pack[0, CHUNK:] = picked[:, :128]
+    pack[1, CHUNK:] = picked[:, 128:]
+
+    right, left = lax.rem(gx + 1, ngx), lax.rem(gx + ngx - 1, ngx)
+
+    def to_right(src, dst, sems, recvs):
+        return remote(src, dst, sems.at[0], recvs.at[0], (mem, right, gy))
+
+    def to_left(src, dst, sems, recvs):
+        return remote(src, dst, sems.at[1], recvs.at[1], (mem, left, gy))
+
+    def exchange_lon(a_src, b_src, dst, sems, recvs, wait=True):
+        a, b = to_right(a_src, dst.at[0], sems, recvs), to_left(b_src, dst.at[1], sems, recvs)
+
+        @pl.when(has_r)
+        def _():
+            a.start()
+
+        @pl.when(has_l)
+        def _():
+            b.start()
+
+        if wait:
+            finish_lon(a, b)
+
+    def finish_lon(a, b):
+        @pl.when(has_l)
+        def _():
+            a.wait_recv()
+
+        @pl.when(has_r)
+        def _():
+            b.wait_recv()
+
+        @pl.when(has_r)
+        def _():
+            a.wait_send()
+
+        @pl.when(has_l)
+        def _():
+            b.wait_send()
+
+    exchange_lon(pack.at[0], pack.at[1], side, as_, ar, False)
     pump(4)
 
     main = tap_of(jnp.abs(px - pa)) - west * tap_of(px + pa + 2) - east * tap_of(256 - px - pa)
@@ -338,6 +354,9 @@
 
     matrices(0, 8)
     pump(5)
+    matrices(8, CHUNKS)
+    pump(6)
+    pump(7)
     for j in range(1, ngx):
         o1_in(j).wait_recv()
 
@@ -357,10 +376,6 @@
     for j in range(1, ngy):
         o2(j).start()
     rb[gy] = tb[:, pl.ds(pl.multiple_of(gy * 8, 8), 8), :]
-    pump(6)
-    matrices(8, CHUNKS)
-    pump(7)
-
     def operator(q):
         turned = rb[q * 2 : q * 2 + 2].reshape(128, 128).T
         for g in range(4):
@@ -458,15 +473,21 @@
         yh_s[CHUNK:] = wide[:, 128:]
         accumulate(y_s, CHUNK, 1, lambda start: xb_rows(320 + start))
 
-    lane192 = iota((192, 128), 1)
     lane16 = iota((16, 128), 1)
+    group16, place16 = lane16 >> 3, lane16 & 7
 
     def around(x):
         for s in (8, 16, 32, 64):
             x = x + pltpu.roll(x, s, 1)
         return x
 
+    def turn(x, s):
+        s = s % 128
+        return pltpu.roll(x, s, 1) if s else x
+
     def reduce_and_observe(it):
+        whole = remote(eb.at[pl.ds(16, 192)], f_mem.at[it], bs.at[it, 0], br.at[it, 0], (1 - mem, gx, gy))
+        whole.start()
         for c8 in range(2):
             acc = [jnp.zeros((8, 128), f32) for _ in range(12)]
             for k in range(5):
@@ -477,72 +498,55 @@
             for row in range(12):
                 eh_s[row * 16 + c8 * 8 : row * 16 + c8 * 8 + 8] = acc[row]
         eh = around(eh_s[...])
-        e = eb[16:208]
-        msend[...] = jnp.where(
-            lane192 < 8,
-            pltpu.roll(eh, 124, 1),
-            jnp.where(lane192 >= 120, pltpu.roll(eh, 4, 1), jnp.where(lane192 == 16, pltpu.roll(e, 16, 1), 0.0)),
-        )
-        exchange_lon(msend, msend, mrecv.at[it], ms.at[it], mr.at[it])
-        m_l, m_r = mrecv[it, 0], mrecv[it, 1]
-        eb[16:208] = e + jnp.where(lane192 < 4, m_l, 0.0) + jnp.where(lane192 >= 124, m_r, 0.0)
-        beyond = pltpu.roll(m_r, 112, 1) + msend[...]
-        xv = jnp.zeros((16, 128), f32)
+        halo, edge = jnp.zeros((16, 128), f32), jnp.zeros((16, 128), f32)
         for row in range(12):
-            b = beyond[row * 16 : row * 16 + 16]
-            xv = xv + jnp.where(lane16 == row, pltpu.roll(b, row, 1) if row else b, 0.0)
+            at = row * 16
+            halo = jnp.where(group16 == row, eh[at : at + 16], halo)
+            edge = jnp.where(lane16 == 8 * row + 4, turn(eb[16 + at : 32 + at], 8 * row + 4), edge)
+        msend[0:16] = halo
+        msend[16:32] = edge
+
+        def columns():
+            out = []
+            for flip in range(2):
+                m = mem if flip == 0 else 1 - mem
+                out.append((has_r, has_l, remote(msend, mrecv.at[it, 0, mem], ms.at[it, flip], mr.at[it, flip], (m, right, gy))))
+                out.append((has_l, has_r, remote(msend, mrecv.at[it, 1, mem], ms.at[it, 2 + flip], mr.at[it, 2 + flip], (m, left, gy))))
+            out.append((None, None, remote(msend, mrecv.at[it, 2, 0], ms.at[it, 4], mr.at[it, 4], (1 - mem, gx, gy))))
+            return out
+
+        run([(c, x) for c, _, x in columns()], "start")
+        run([(c, x) for _, c, x in columns()] + [(None, whole)], "wait_recv")
+        run([(c, x) for c, _, x in columns()] + [(None, whole)], "wait_send")
+        m_l = mrecv[it, 0, 0] + mrecv[it, 0, 1]
+        m_r = mrecv[it, 1, 0] + mrecv[it, 1, 1]
+        m_o = halo + mrecv[it, 2, 0, 0:16]
+        for row in range(12):
+            at = row * 16
+            e = eb[16 + at : 32 + at] + f_mem[it, at : at + 16]
+            e = e + jnp.where(lane16 < 4, turn(m_l[0:16], -8 * row - 4), 0.0)
+            e = e + jnp.where(lane16 >= 124, turn(m_r[0:16], 124 - 8 * row), 0.0)
+            eb[16 + at : 32 + at] = e
+        xv = jnp.where((place16 == 4) & (lane16 < 96), m_r[16:32] + m_o, 0.0)
         eb[0:16] = xv
         eb[208:224] = xv
 
-        def sends():
-            out = []
-            n = 0
-            for flip in range(2):
-                m = mem if flip == 0 else 1 - mem
-                out.append((gy < ngy - 1, remote(eb.at[pl.ds(144, 80)], f_dn.at[it, mem], bs.at[it, n], br.at[it, n], (m, gx, lax.rem(gy + 1, ngy)))))
-                out.append((gy > 0, remote(eb.at[pl.ds(0, 96)], f_up.at[it, mem], bs.at[it, n + 1], br.at[it, n + 1], (m, gx, lax.rem(gy + ngy - 1, ngy)))))
-                out.append((gy > 1, remote(eb.at[pl.ds(0, 32)], f_up2.at[it, mem], bs.at[it, n + 2], br.at[it, n + 2], (m, gx, lax.rem(gy + ngy - 2, ngy)))))
-                n += 3
-            out.append((None, remote(eb.at[pl.ds(80, 80)], f_mem.at[it, pl.ds(0, 80)], bs.at[it, 6], br.at[it, 6], (1 - mem, gx, gy))))
-            out.append((None, remote(eb.at[pl.ds(208, 16)], f_mem.at[it, pl.ds(80, 16)], bs.at[it, 7], br.at[it, 7], (1 - mem, gx, gy))))
-            return out
-
-        def receives():
-            out = []
-            n = 0
-            for flip in range(2):
-                m = mem if flip == 0 else 1 - mem
-                out.append((gy > 0, remote(eb.at[pl.ds(144, 80)], f_dn.at[it, m], bs.at[it, n], br.at[it, n], (mem, gx, gy))))
-                out.append((gy < ngy - 1, remote(eb.at[pl.ds(0, 96)], f_up.at[it, m], bs.at[it, n + 1], br.at[it, n + 1], (mem, gx, gy))))
-                out.append((gy < ngy - 2, remote(eb.at[pl.ds(0, 32)], f_up2.at[it, m], bs.at[it, n + 2], br.at[it, n + 2], (mem, gx, gy))))
-                n += 3
-            out.append((None, remote(eb.at[pl.ds(80, 80)], f_mem.at[it, pl.ds(0, 80)], bs.at[it, 6], br.at[it, 6], (mem, gx, gy))))
-            out.append((None, remote(eb.at[pl.ds(208, 16)], f_mem.at[it, pl.ds(80, 16)], bs.at[it, 7], br.at[it, 7], (mem, gx, gy))))
-            return out
-
-        run(sends(), "start")
-        run(receives(), "wait_recv")
-        run(sends(), "wait_send")
-
-        def block_sum(own, own_xv, m):
-            rows = []
-            for r in range(5):
-                t = own(r) + f_up[it, m, (r + 1) * 16 : (r + 2) * 16]
-                if r < 4:
-                    t = t + f_dn[it, m, r * 16 : r * 16 + 16]
-                else:
-                    t = t + f_up2[it, m, 16:32]
-                rows.append(t)
-            x = own_xv + pltpu.roll(f_dn[it, m, 64:80], 124, 1) + pltpu.roll(f_up[it, m, 0:16], 4, 1)
-            x = x + pltpu.roll(jnp.where(lane16 == 0, f_up2[it, m, 0:16], 0.0), 8, 1)
-            return rows, x
-
-        mine, x_mine = block_sum(lambda r: eb[80 + r * 16 : 96 + r * 16], eb[208:224], mem)
-        theirs, x_theirs = block_sum(lambda r: f_mem[it, r * 16 : r * 16 + 16], f_mem[it, 80:96], 1 - mem)
-        x = (x_mine + x_theirs) * ENS
+        def rows_out():
+            return [
+                (gy < ngy - 1, gy > 0, remote(eb.at[pl.ds(144, 80)], f_dn.at[it], bs.at[it, 1], br.at[it, 1], (1 - mem, gx, lax.rem(gy + 1, ngy)))),
+                (gy > 0, gy < ngy - 1, remote(eb.at[pl.ds(0, 96)], f_up.at[it], bs.at[it, 2], br.at[it, 2], (1 - mem, gx, lax.rem(gy + ngy - 1, ngy)))),
+                (gy > 1, gy < ngy - 2, remote(eb.at[pl.ds(0, 32)], f_up2.at[it], bs.at[it, 3], br.at[it, 3], (mem, gx, lax.rem(gy + ngy - 2, ngy)))),
+            ]
+
+        run([(c, x) for c, _, x in rows_out()], "start")
+        run([(c, x) for _, c, x in rows_out()], "wait_recv")
+        run([(c, x) for c, _, x in rows_out()], "wait_send")
+        x = xv + turn(f_dn[it, 64:80], -32) + turn(f_up[it, 0:16], 32)
+        x = (x + turn(jnp.where(lane16 == 4, f_up2[it, 0:16], 0.0), 64)) * ENS
         for r in range(5):
-            dx = (mine[r] + theirs[r]) * ENS
-            moved = jnp.where(lane16 == 127, pltpu.roll(x, 127 - (r + 4), 1), pltpu.roll(dx, 127, 1))
+            dx = eb[80 + r * 16 : 96 + r * 16] + f_up[it, (r + 1) * 16 : (r + 2) * 16]
+            dx = (dx + (f_dn[it, r * 16 : r * 16 + 16] if r < 4 else f_up2[it, 16:32])) * ENS
+            moved = jnp.where(lane16 == 127, turn(x, 127 - 8 * (r + 4) - 4), turn(dx, 127))
             if it == ITERS - 1 and r < 4:
                 inc_out[every4(r), :] = dx[:8]
                 inc_out[every4(32 + r), :] = dx[8:]
@@ -566,47 +570,58 @@
 
         lane80 = iota((80, 128), 1)
         g0, g1 = gacc[0:80], gacc[80:160]
-        g5 = g0 + jnp.where(lane80 == 0, 0.0, pltpu.roll(g1, 1, 1))
-        nsend[...] = jnp.where(lane80 == 64, pltpu.roll(g1, 65, 1), g5)
-        exchange_lon(nsend, nsend, nrecv.at[it], ns.at[it], nr.at[it])
-        n_l, n_r = nrecv[it, 0], nrecv[it, 1]
-        gb[16:96] = g5 + jnp.where(lane80 == 0, pltpu.roll(n_l, 64, 1), 0.0)
-        halo = jnp.where(
-            lane80 < 4,
-            pltpu.roll(n_l, 4, 1),
-            jnp.where(lane80 < 8, pltpu.roll(n_r, 4, 1) + jnp.where(lane80 == 4, pltpu.roll(g1, 5, 1), 0.0), 0.0),
-        )
-        ghv = halo[0:16]
-        for r in range(1, 5):
-            ghv = ghv + pltpu.roll(halo[r * 16 : r * 16 + 16], 8 * r, 1)
-        gb[0:16] = ghv
-        gb[96:112] = ghv
-
-        def sends_g():
-            return [
-                (gy < ngy - 1, remote(gb.at[pl.ds(16, 96)], g_dn.at[it], ds_.at[it, 0], dr.at[it, 0], (1 - mem, gx, lax.rem(gy + 1, ngy)))),
-                (gy > 0, remote(gb.at[pl.ds(0, 80)], g_up.at[it], ds_.at[it, 1], dr.at[it, 1], (1 - mem, gx, lax.rem(gy + ngy - 1, ngy)))),
-                (gy < ngy - 2, remote(gb.at[pl.ds(80, 32)], g_dn2.at[it], ds_.at[it, 2], dr.at[it, 2], (mem, gx, lax.rem(gy + 2, ngy)))),
+        gb[16:96] = g0 + jnp.where(lane80 == 0, 0.0, turn(g1, 1))
+        sides = jnp.zeros((16, 128), f32)
+        for r in range(5):
+            at = r * 16
+            g5 = gb[16 + at : 32 + at]
+            both = jnp.where(place16 < 4, turn(g5, 8 * r + 4), turn(g5, 8 * r + 4))
+            sides = jnp.where(group16 == r, both, sides)
+            sides = jnp.where(lane16 == 64 + 8 * r, turn(g1[at : at + 16], 64 + 8 * r - 127), sides)
+        gb[0:16] = sides
+        gb[96:112] = sides
+
+        def terms():
+            out = [
+                (gy < ngy - 1, gy > 0, remote(gb.at[pl.ds(16, 96)], g_dn.at[it], ds_.at[it, 0], dr.at[it, 0], (1 - mem, gx, lax.rem(gy + 1, ngy)))),
+                (gy > 0, gy < ngy - 1, remote(gb.at[pl.ds(0, 80)], g_up.at[it], ds_.at[it, 1], dr.at[it, 1], (1 - mem, gx, lax.rem(gy + ngy - 1, ngy)))),
+                (gy < ngy - 2, gy > 1, remote(gb.at[pl.ds(80, 32)], g_dn2.at[it], ds_.at[it, 2], dr.at[it, 2], (mem, gx, lax.rem(gy + 2, ngy)))),
             ]
-
-        def receives_g():
-            both = sends_g()
-            return [(gy > 0, both[0][1]), (gy < ngy - 1, both[1][1]), (gy > 1, both[2][1])]
-
-        run(sends_g(), "start")
-        run(receives_g(), "wait_recv")
-        run(sends_g(), "wait_send")
+            for n, (m, step) in enumerate(((mem, 0), (1 - mem, 1), (1 - mem, -1), (mem, 2))):
+                to, of = gy + step, gy - step
+                there, here = (to >= 0) & (to < ngy), (of >= 0) & (of < ngy)
+                row = lax.rem(to + ngy, ngy)
+                for k, (x, c, d) in enumerate(((right, has_r, has_l), (left, has_l, has_r))):
+                    copy = remote(gb.at[pl.ds(0, 16)], nrecv.at[it, n, k], ns.at[it, 2 * n + k], nr.at[it, 2 * n + k], (m, x, row))
+                    out.append((c & there, d & here, copy))
+            return out
+
+        run([(c, x) for c, _, x in terms()], "start")
+        run([(c, x) for _, c, x in terms()], "wait_recv")
+        run([(c, x) for c, _, x in terms()], "wait_send")
+        beside = [nrecv[it, n] for n in range(4)]
+        centre = [sides, g_dn[it, 80:96], g_up[it, 0:16], g_dn2[it, 16:32]]
+
+        def halos(n):
+            own = jnp.where((place16 == 4) & (lane16 < 40), turn(centre[n], -60), 0.0)
+            return jnp.where(place16 < 4, beside[n][0], beside[n][1] + own)
+
+        def row_of(n, v, r):
+            return v + jnp.where(lane16 == 0, turn(beside[n][0], -64 - 8 * r), 0.0)
+
+        halo_own, halo_dn, halo_up, halo_dn2 = [halos(n) for n in range(4)]
 
         def ext(v, r):
-            return jnp.where(lane16 < 8, pltpu.roll(v, 128 - 8 * r, 1) if r else v, 0.0)
+            return jnp.where(lane16 < 8, turn(v, -8 * r), 0.0)
 
         for r in range(4):
-            below, own, above = g_dn[it, r * 16 : r * 16 + 16], gb[16 + r * 16 : 32 + r * 16], g_up[it, 16 + r * 16 : 32 + r * 16]
-            hb, ho, ha = ext(g_dn[it, 80:96], r), ext(ghv, r), ext(g_up[it, 0:16], r)
+            at = r * 16
+            below, own, above = row_of(1, g_dn[it, at : at + 16], r), row_of(0, gb[16 + at : 32 + at], r), row_of(2, g_up[it, 16 + at : 32 + at], r)
+            hb, ho, ha = ext(halo_dn, r), ext(halo_own, r), ext(halo_up, r)
             if r == 0:
-                below, hb = below + g_dn2[it, 0:16], hb + ext(g_dn2[it, 16:32], 4)
-                own, ho = own + g_dn[it, 64:80], ho + ext(g_dn[it, 80:96], 4)
-                above, ha = above + gb[80:96], ha + ext(ghv, 4)
+                below, hb = below + row_of(3, g_dn2[it, 0:16], 4), hb + ext(halo_dn2, 4)
+                own, ho = own + row_of(1, g_dn[it, 64:80], 4), ho + ext(halo_dn, 4)
+                above, ha = above + row_of(0, gb[80:96], 4), ha + ext(halo_own, 4)
             for n, (v, h) in enumerate(((below, hb), (own, ho), (above, ha))):
                 at = n * 64 + r * 16
                 gx_s[at : at + 16] = v
@@ -663,11 +678,16 @@
     fetch.wait()
     for i in range(8, CHUNKS):
         pump(i)
-        if i == 10:
+        if i == 9:
+            finish_lon(to_right(pack.at[0], side.at[0], as_, ar), to_left(pack.at[1], side.at[1], as_, ar))
+            xb[OWN, :320] = side[0] + side[1]
+            direct_x().start()
+        if i == 13:
             for j in range(1, ngy):
                 o2_in(j).wait_recv()
-        if i >= 11 and i < 15:
-            operator(i - 11)
+        if i >= 13 and i < 15:
+            operator(2 * i - 26)
+            operator(2 * i - 25)
         if i < 15:
 
             @pl.loop(2 * (i - 8), 2 * (i - 8) + 2)
@@ -761,14 +781,13 @@
         V((2, 320, 128), bf16),
         V((224, 128), f32),
         V((192, 128), f32),
-        V((192, 128), f32),
-        V((ITERS, 2, 192, 128), f32),
-        V((ITERS, 2, 80, 128), f32),
-        V((ITERS, 2, 96, 128), f32),
-        V((ITERS, 2, 32, 128), f32),
+        V((32, 128), f32),
+        V((ITERS, 3, 2, 32, 128), f32),
+        V((ITERS, 80, 128), f32),
         V((ITERS, 96, 128), f32),
-        V((80, 128), f32),
-        V((ITERS, 2, 80, 128), f32),
+        V((ITERS, 32, 128), f32),
+        V((ITERS, 192, 128), f32),
+        V((ITERS, 4, 2, 16, 128), f32),
         V((112, 128), f32),
         V((ITERS, 96, 128), f32),
         V((ITERS, 80, 128), f32),
@@ -789,9 +808,9 @@
         dma((CHUNKS + 1,)), dma((CHUNKS + 1,)), dma((CHUNKS + 1,)), dma((CHUNKS + 1,)),
         dma((2,)), dma((2,)),
         dma((8,)), dma((8,)), dma((8,)), dma((8,)),
-        dma((ITERS, 2)), dma((ITERS, 2)),
+        dma((ITERS, 5)), dma((ITERS, 5)),
+        dma((ITERS, 4)), dma((ITERS, 4)),
         dma((ITERS, 8)), dma((ITERS, 8)),
-        dma((ITERS, 2)), dma((ITERS, 2)),
         dma((ITERS, 3)), dma((ITERS, 3)),
         dma((1,)), dma((CHUNKS,)),
     ]

time: 151 us -> 137 us (0.907)
  Pallas kernels: 146 us -> 132 us
    pallas_call x1, Pallas kernels: 146 us -> 132 us  [per_device(): pl.pallas_call(body, out_shape=(jax.ShapeDtypeStruct((rows, 128), f32), j...]
where the time goes in v3:
time: 137 us
  Pallas kernels  132 us (96%)
  local copies, waits for them, and re-layouts  4.47 us (3%)
    pallas_call x1, Pallas kernels, per_device(): pl.pallas_call(body, out_shape=(jax.ShapeDtypeStruct((rows, 128), f32), j...  132 us
    unnamed x7, local copies, waits for them, and re-layouts  4.47 us

profile of v3, /device:TPU:1, one launch (start us, length us, event | category | flops | bytes accessed | tf_op | source)
XLA Modules:
  0.0 136.7 jit_solution(11131396960713839952)
XLA Ops:
  0.6 131.5 %assimilate.1 = (f32[4096,128]{1,0:T(8,128)}, f32[64,128]{1,0:T(8,128)}, f32[64,128]{1,0:T(8,128)}) custom-call(f32[4096,128]{1,0:T(8,128)} %bitcast.12, bf16[4096,128]{1,0:T(8,128)(2,1)} %bitcast.14, f32[64,128]{1,0:T(8,128)} %bitcast.16, f32[64,128]{1,0:T(8,128)} %bitcast.17, f32[16,1024]{1,0:T(8,128)} %bitcast.15, f32[4,1024]{1,0:T(4,128)} %interp.1, ...), custom_call_target="tpu_custom_call" | custom-call | tf_op jit(solution)/shard_map/assimilate/pallas_call | solution.py:817
  132.2 0.0 copy-start.1
  132.2 0.0 copy-start
  132.2 3.2 %copy.16 = f32[64,2,8,4,128]{4,3,2,1,0:T(4,128)} copy(f32[64,2,8,4,128]{4,3,2,1,0:T(4,128)} %bitcast.13) | data formatting | bytes 4194304
  135.4 0.0 copy-done.1
  135.4 0.6 copy.17
  136.1 0.0 copy-done
  136.1 0.6 copy.18
Async XLA Ops:
  132.2 3.3 %copy-start.1 = (f32[64,128]{1,0:T(8,128)S(1)}, f32[64,128]{1,0:T(8,128)}, u32[]{:S(2)}) copy-start(f32[64,128]{1,0:T(8,128)} %get-tuple-element.7) | copy-start | bytes 98308
  132.2 3.9 %copy-start = (f32[64,128]{1,0:T(8,128)S(1)}, f32[64,128]{1,0:T(8,128)}, u32[]{:S(2)}) copy-start(f32[64,128]{1,0:T(8,128)} %get-tuple-element.8) | copy-start | bytes 98308

commit v4 on v3

--- a/solution.py
+++ b/solution.py
@@ -72,7 +72,7 @@
 def body(
     alpha, pert, stat, sig, coef, interp, oval, owgt, tile, cell,
     alpha_out, stat_out, inc_out,
-    own, work, buf, xb, pack, side, wf, wa, y_s, yh_s, vh_s, eb, eh_s, msend, mrecv,
+    own, work, buf, xb, pack, side, wf, wa, y_a, y_b, y_c, yh_s, vh_s, eb, eh_s, msend, mrecv,
     f_dn, f_up, f_up2, f_mem, nrecv, gb, g_dn, g_up, g_dn2, gx_s, gh_s,
     feat, ft, key_s, sb, tb, rb, qt, cm, ov, lh, gacc,
     ps, pr, fs, fr, as_, ar, o1s, o1r, o2s, o2r, ms, mr, bs, br, ns, nr, ds_, dr, al, ao,
@@ -344,13 +344,14 @@
             j = pa - 8 * i
             d = jnp.where(j < 4, px + 4 - j, 124 + j - px)
             h_hi, h_lo = split2(jnp.where((j >= 0) & (j < 8), tap_of(d), 0.0))
-            wf[i, 0] = jnp.concatenate([main_hi, h_hi], axis=1)
-            wf[i, 1] = jnp.concatenate([main_lo, h_lo], axis=1)
+            wf[i, 0:128] = jnp.concatenate([main_hi, h_hi], axis=1)
+            wf[i, 128:256] = jnp.concatenate([main_hi, h_hi], axis=1)
+            wf[i, 256:384] = jnp.concatenate([main_lo, h_lo], axis=1)
             j = px - 8 * i
             d = jnp.where(j < 4, pa + 4 - j, 124 + j - pa)
             h_hi, h_lo = split2(jnp.where((j >= 0) & (j < 8), tap_of(d), 0.0))
-            wa[i, 0] = jnp.concatenate([main_hi, h_hi], axis=0)
-            wa[i, 1] = jnp.concatenate([main_lo, h_lo], axis=0)
+            wa[i, :, :128] = jnp.concatenate([main_hi, h_hi], axis=0)
+            wa[i, :, 128:] = jnp.concatenate([main_lo, h_lo], axis=0)
 
     matrices(0, 8)
     pump(5)
@@ -439,21 +440,22 @@
     def xb_rows(start):
         return [xb[b, every4(start + r), :] for b in (BELOW, OWN, ABOVE) for r in range(4)]
 
-    def lon(x, w, i):
+    def lon(x, i):
         hi, lo = split2(x)
-        return dot(hi, w[i, 0]) + dot(lo, w[i, 0]) + dot(hi, w[i, 1])
+        return dot(jnp.concatenate([hi, lo], axis=1), wf[i, 0:256]) + dot(hi, wf[i, 256:384])
 
     def eb_at(row, c8):
         return pl.ds((row + 1) * 16 + c8 * 8, 8)
 
-    def accumulate(y, first, count, rows):
+    def accumulate(parts, count):
         for c8 in range(2):
             acc = [eb[eb_at(row, c8), :] for row in range(12)]
-            for k in range(count):
-                start = k * 64 + c8 * 32
-                z = lat_out([y[every4(first + start + r), :] for r in range(4)])
-                p = rows(start)
-                acc = [acc[row] + z[row] * p[row] for row in range(12)]
+            for y, rows in parts:
+                for k in range(count):
+                    start = k * 64 + c8 * 32
+                    z = lat_out([y[every4(start + r), :] for r in range(4)])
+                    p = rows(start)
+                    acc = [acc[row] + z[row] * p[row] for row in range(12)]
             for row in range(12):
                 eb[eb_at(row, c8), :] = acc[row]
 
@@ -461,17 +463,21 @@
         eb[...] = jnp.zeros(eb.shape, f32)
         yh_s[...] = jnp.zeros(yh_s.shape, f32)
 
-    def member_chunk(src, i):
-        wide = lon(src[rows_of(i), :], wf, i)
-        y_s[:CHUNK] = wide[:, :128]
-        yh_s[:CHUNK] += wide[:, 128:]
-        accumulate(y_s, 0, 4, lambda start: pert_rows(pl.multiple_of(i * CHUNK, CHUNK) + start))
+    def rows_from(i):
+        return lambda start: pert_rows(pl.multiple_of(i * CHUNK, CHUNK) + start)
+
+    def member_pair(i, xs):
+        for y, x, n in zip((y_a, y_b), xs, (i, i + 1)):
+            wide = lon(x, n)
+            y[...] = wide[:, :128]
+            yh_s[:CHUNK] += wide[:, 128:]
+        accumulate([(y_a, rows_from(i)), (y_b, rows_from(i + 1))], 4)
 
     def static_chunk(src):
-        wide = lon(src[...] * jnp.where(mem == 0, 1.0, 0.0), wf, 0)
-        y_s[CHUNK:] = wide[:, :128]
+        wide = lon(src[...] * jnp.where(mem == 0, 1.0, 0.0), 0)
+        y_c[...] = wide[:, :128]
         yh_s[CHUNK:] = wide[:, 128:]
-        accumulate(y_s, CHUNK, 1, lambda start: xb_rows(320 + start))
+        accumulate([(y_c, lambda start: xb_rows(320 + start))], 1)
 
     lane16 = iota((16, 128), 1)
     group16, place16 = lane16 >> 3, lane16 & 7
@@ -552,8 +558,8 @@
                 inc_out[every4(32 + r), :] = dx[8:]
             for n, v in ((0, dx), (1, moved)):
                 hi, lo = split2(v)
-                lh[0, n * 80 + r * 16 : n * 80 + r * 16 + 16] = hi
-                lh[1, n * 80 + r * 16 : n * 80 + r * 16 + 16] = lo
+                lh[n * 80 + r * 16 : n * 80 + r * 16 + 16, :128] = hi
+                lh[n * 80 + r * 16 : n * 80 + r * 16 + 16, 128:] = lo
 
         gacc[...] = jnp.zeros(gacc.shape, f32)
 
@@ -561,12 +567,13 @@
         def _(n):
             at = pl.ds(pl.multiple_of(n * 256, 256), 256)
             c = cm[:, at]
-            u = dot(lh[0], c) + dot(lh[1], c)
+            u = dot(lh[...], jnp.concatenate([c, c], axis=0))
             q = qt[:, at]
             hx = jnp.sum(q * u, axis=0, keepdims=True)
             misfit = ov[1:2, at] * (hx - ov[0:1, at])
             hi, lo = split2(q * misfit)
-            gacc[...] += dot_nt(hi, c) + dot_nt(lo, c)
+            both = dot_nt(jnp.concatenate([hi, lo], axis=0), c)
+            gacc[...] += both[:160] + both[160:]
 
         lane80 = iota((80, 128), 1)
         g0, g1 = gacc[0:80], gacc[80:160]
@@ -575,8 +582,7 @@
         for r in range(5):
             at = r * 16
             g5 = gb[16 + at : 32 + at]
-            both = jnp.where(place16 < 4, turn(g5, 8 * r + 4), turn(g5, 8 * r + 4))
-            sides = jnp.where(group16 == r, both, sides)
+            sides = jnp.where(group16 == r, turn(g5, 8 * r + 4), sides)
             sides = jnp.where(lane16 == 64 + 8 * r, turn(g1[at : at + 16], 64 + 8 * r - 127), sides)
         gb[0:16] = sides
         gb[96:112] = sides
@@ -647,42 +653,57 @@
             else:
                 pl.when(condition)(lambda copy=copy: getattr(copy, what)())
 
-    def gradient(first, count, halo, rows, i):
+    def gradient_rows(parts, count):
         for c8 in range(2):
             g = [gx_s[row * 16 + c8 * 8 : row * 16 + c8 * 8 + 8] for row in range(12)]
-            for k in range(count):
-                start = k * 64 + c8 * 32
-                p = rows(start)
-                v = lat_in([p[row] * g[row] for row in range(12)])
-                for r in range(4):
-                    y_s[every4(first + start + r), :] = v[r]
-        n = count * 64
-        hi, lo = split2(y_s[first : first + n])
+            for y, rows in parts:
+                for k in range(count):
+                    start = k * 64 + c8 * 32
+                    p = rows(start)
+                    v = lat_in([p[row] * g[row] for row in range(12)])
+                    for r in range(4):
+                        y[every4(start + r), :] = v[r]
+
+    def gradient(y, halo, i):
+        n = y.shape[0]
+        hi, lo = split2(y[...])
         hi = jnp.concatenate([hi, vh_s[0, halo : halo + n]], axis=1)
         lo = jnp.concatenate([lo, vh_s[1, halo : halo + n]], axis=1)
-        return dot(hi, wa[i, 0]) + dot(lo, wa[i, 0]) + dot(hi, wa[i, 1])
-
-    def member_step(i):
-        u = gradient(0, 4, 0, lambda start: pert_rows(pl.multiple_of(i * CHUNK, CHUNK) + start), i)
-        work[rows_of(i), :] = (1.0 - DESCENT) * work[rows_of(i), :] - (DESCENT * ENS) * u
+        both = dot(hi, wa[i])
+        return both[:, :128] + both[:, 128:] + dot(lo, wa[i, :, :128])
+
+    def member_steps(i):
+        gradient_rows([(y_a, rows_from(i)), (y_b, rows_from(i + 1))], 4)
+        out = []
+        for y, n in ((y_a, i), (y_b, i + 1)):
+            x = (1.0 - DESCENT) * work[rows_of(n), :] - (DESCENT * ENS) * gradient(y, 0, n)
+            work[rows_of(n), :] = x
+            out.append(x)
+        return out
 
     def done(i):
         return pltpu.make_async_copy(work.at[rows_of(i)], alpha_out.at[rows_of(i)], ao.at[i])
 
     def static_step(src):
-        u = gradient(CHUNK, 1, CHUNK, lambda start: xb_rows(320 + start), 0)
-        stat_out[...] = (1.0 - DESCENT) * src[...] - (DESCENT * ENS) * u
+        gradient_rows([(y_c, lambda start: xb_rows(320 + start))], 1)
+        stat_out[...] = (1.0 - DESCENT) * src[...] - (DESCENT * ENS) * gradient(y_c, CHUNK, 0)
 
     clear()
 
     fetch.wait()
     for i in range(8, CHUNKS):
         pump(i)
-        if i == 9:
+        if i == 8:
             finish_lon(to_right(pack.at[0], side.at[0], as_, ar), to_left(pack.at[1], side.at[1], as_, ar))
             xb[OWN, :320] = side[0] + side[1]
             direct_x().start()
         if i == 13:
+            arrival_x().wait_recv()
+
+            @pl.when(has_f)
+            def _():
+                forward_x().start()
+
             for j in range(1, ngy):
                 o2_in(j).wait_recv()
         if i >= 13 and i < 15:
@@ -690,21 +711,14 @@
             operator(2 * i - 25)
         if i < 15:
 
-            @pl.loop(2 * (i - 8), 2 * (i - 8) + 2)
-            def _(n):
-                landed(n)
-                member_chunk(work, n)
-
-    arrival_x().wait_recv()
-
-    @pl.when(has_f)
-    def _():
-        forward_x().start()
-
-    @pl.loop(CHUNKS - 2, CHUNKS)
-    def _(i):
-        landed(i)
-        member_chunk(work, i)
+            n = 2 * (i - 8)
+            landed(n)
+            landed(n + 1)
+            member_pair(n, [work[rows_of(n), :], work[rows_of(n + 1), :]])
+
+    landed(CHUNKS - 2)
+    landed(CHUNKS - 1)
+    member_pair(CHUNKS - 2, [work[rows_of(CHUNKS - 2), :], work[rows_of(CHUNKS - 1), :]])
 
     @pl.when(has_b)
     def _():
@@ -714,19 +728,19 @@
     reduce_and_observe(0)
     clear()
 
-    @pl.loop(0, CHUNKS)
+    @pl.loop(0, CHUNKS // 2)
     def _(i):
-        member_step(i)
-        member_chunk(work, i)
+        member_pair(2 * i, member_steps(2 * i))
 
     static_step(stat)
     static_chunk(stat_out)
     reduce_and_observe(1)
 
-    @pl.loop(0, CHUNKS)
+    @pl.loop(0, CHUNKS // 2)
     def _(i):
-        member_step(i)
-        done(i).start()
+        member_steps(2 * i)
+        done(2 * i).start()
+        done(2 * i + 1).start()
 
     static_step(stat_out)
     for i in range(CHUNKS):
@@ -746,6 +760,20 @@
         o1(j).wait_send()
     for j in range(1, ngy):
         o2(j).wait_send()
+
+
+def hand_over(a, b, c, a_out, b_out, c_out, a_s, b_s, c_s, ins, outs):
+    parts = [pl.ds(n * (a.shape[0] // 8), a.shape[0] // 8) for n in range(8)]
+    moves = [(a.at[p], a_s.at[p], a_out.at[p]) for p in parts] + [(b, b_s, b_out), (c, c_s, c_out)]
+    fetches = [pltpu.make_async_copy(x, y, ins.at[n]) for n, (x, y, _) in enumerate(moves)]
+    stores = [pltpu.make_async_copy(y, z, outs.at[n]) for n, (_, y, z) in enumerate(moves)]
+    for copy in fetches:
+        copy.start()
+    for fetch, store in zip(fetches, stores):
+        fetch.wait()
+        store.start()
+    for copy in stores:
+        copy.wait()
 
 
 def per_device(
@@ -774,9 +802,11 @@
         V((3, 384, 128), f32),
         V((2, 320, 128), f32),
         V((2, 320, 128), f32),
-        V((CHUNKS, 2, 128, 256), bf16),
-        V((CHUNKS, 2, 256, 128), bf16),
-        V((320, 128), f32),
+        V((CHUNKS, 384, 256), bf16),
+        V((CHUNKS, 256, 256), bf16),
+        V((CHUNK, 128), f32),
+        V((CHUNK, 128), f32),
+        V((64, 128), f32),
         V((320, 128), f32),
         V((2, 320, 128), bf16),
         V((224, 128), f32),
@@ -803,7 +833,7 @@
         V((160, 2048), f32),
         V((128, 2048), bf16),
         V((8, 2048), f32),
-        V((2, 160, 128), bf16),
+        V((160, 256), bf16),
         V((160, 128), f32),
         dma((CHUNKS + 1,)), dma((CHUNKS + 1,)), dma((CHUNKS + 1,)), dma((CHUNKS + 1,)),
         dma((2,)), dma((2,)),
@@ -829,6 +859,15 @@
             collective_id=0, has_side_effects=True, vmem_limit_bytes=56 << 20
         ),
     )(*args)
+    anywhere = pl.BlockSpec(memory_space=pl.ANY)
+    outs = pl.pallas_call(
+        hand_over,
+        out_shape=tuple(jax.ShapeDtypeStruct(x.shape, f32) for x in outs),
+        in_specs=[anywhere] * 3,
+        out_specs=(anywhere,) * 3,
+        scratch_shapes=[V(x.shape, f32) for x in outs] + [dma((10,)), dma((10,))],
+        name="hand_over",
+    )(*outs)
     return (
         outs[0].reshape(alpha.shape),
         outs[1].reshape(static_control.shape),

time: 137 us -> 122 us (0.89)
  Pallas kernels: 132 us -> 122 us
  local copies, waits for them, and re-layouts: 4.47 us -> 0 us
    pallas_call x1, Pallas kernels: 132 us -> 119 us  [per_device(): pl.pallas_call(body, out_shape=(jax.ShapeDtypeStruct((rows, 128), f32), j...]
    unnamed x7 -> x0, local copies, waits for them, and re-layouts: 4.47 us -> none
    pallas_call x0 -> x1, Pallas kernels: none -> 2.44 us  [per_device(): pl.pallas_call(hand_over, out_shape=tuple((jax.ShapeDtypeStruct(x.shape,...]
where the time goes in v4:
time: 122 us
  Pallas kernels  122 us (100%)
    pallas_call x1, Pallas kernels, per_device(): pl.pallas_call(body, out_shape=(jax.ShapeDtypeStruct((rows, 128), f32), j...  119 us
    pallas_call x1, Pallas kernels, per_device(): pl.pallas_call(hand_over, out_shape=tuple((jax.ShapeDtypeStruct(x.shape,...  2.44 us

profile of v4, /device:TPU:1, one launch (start us, length us, event | category | flops | bytes accessed | tf_op | source)
XLA Modules:
  0.0 122.3 jit_solution(17898309881169049081)
XLA Ops:
  0.6 119.2 %assimilate.1 = (f32[4096,128]{1,0:T(8,128)}, f32[64,128]{1,0:T(8,128)}, f32[64,128]{1,0:T(8,128)}) custom-call(f32[4096,128]{1,0:T(8,128)} %bitcast.12, bf16[4096,128]{1,0:T(8,128)(2,1)} %bitcast.13, f32[64,128]{1,0:T(8,128)} %bitcast.15, f32[64,128]{1,0:T(8,128)} %bitcast.16, f32[16,1024]{1,0:T(8,128)} %bitcast.14, f32[4,1024]{1,0:T(4,128)} %interp.1, ...), custom_call_target="tpu_custom_call" | custom-call | tf_op jit(solution)/shard_map/assimilate/pallas_call | solution.py:847
  119.8 2.4 %hand_over.1 = (f32[4096,128]{1,0:T(8,128)}, f32[64,128]{1,0:T(8,128)}, f32[64,128]{1,0:T(8,128)}) custom-call(f32[4096,128]{1,0:T(8,128)} %get-tuple-element.9.a, f32[64,128]{1,0:T(8,128)} %get-tuple-element.10.b, f32[64,128]{1,0:T(8,128)} %get-tuple-element.11.c), custom_call_target="tpu_custom_call" | custom-call | tf_op jit(solution)/shard_map/hand_over/pallas_call | solution.py:863

commit v5 on v4

--- a/solution.py
+++ b/solution.py
@@ -72,7 +72,7 @@
 def body(
     alpha, pert, stat, sig, coef, interp, oval, owgt, tile, cell,
     alpha_out, stat_out, inc_out,
-    own, work, buf, xb, pack, side, wf, wa, y_a, y_b, y_c, yh_s, vh_s, eb, eh_s, msend, mrecv,
+    own, work, buf, xb, pack, side, wf, wa, y_all, y_a, y_b, y_c, yh_s, vh_s, eb, eh_s, msend, mrecv,
     f_dn, f_up, f_up2, f_mem, nrecv, gb, g_dn, g_up, g_dn2, gx_s, gh_s,
     feat, ft, key_s, sb, tb, rb, qt, cm, ov, lh, gacc,
     ps, pr, fs, fr, as_, ar, o1s, o1r, o2s, o2r, ms, mr, bs, br, ns, nr, ds_, dr, al, ao,
@@ -97,11 +97,13 @@
     def greet(m, x, y):
         pl.semaphore_signal(barrier, inc=1, device_id=(m, lax.rem(x + ngx, ngx), lax.rem(y + ngy, ngy)), device_id_type=MESH)
 
+    greet(mem, gx, partner)
+    for j in range(2, ngy, 2):
+        greet(mem, gx, gy + j)
     for j in range(1, ngx):
         greet(mem, gx + j, gy)
-    for j in range(1, ngy):
-        greet(mem, gx, gy + j)
-    for j in range(ngy):
+    greet(1 - mem, gx, gy)
+    for j in range(1, ngy, 2):
         greet(1 - mem, gx, gy + j)
     for dx in (-1, 1):
         greet(1 - mem, gx + dx, gy)
@@ -109,7 +111,7 @@
             greet(1 - mem, gx + dx, gy + dy)
         for dy in (-2, 2):
             greet(mem, gx + dx, gy + dy)
-    pl.semaphore_wait(barrier, ngx + 2 * ngy - 2 + 10)
+    pl.semaphore_wait(barrier, ngx + ngy + 10)
 
     def remote(src, dst, s, r, device):
         return pltpu.make_async_remote_copy(
@@ -119,100 +121,57 @@
     def rows_of(i):
         return pl.ds(pl.multiple_of(i * CHUNK, CHUNK), CHUNK)
 
-    def direct(i):
-        return remote(own.at[rows_of(i)], buf.at[par, rows_of(i)], ps.at[i], pr.at[i], (mem, gx, partner))
-
-    def arrival(i):
-        return remote(own.at[rows_of(i)], buf.at[1 - par, rows_of(i)], ps.at[i], pr.at[i], (mem, gx, partner))
-
-    def forward(i):
-        return remote(
-            buf.at[1 - par, rows_of(i)], buf.at[par, rows_of(i)], fs.at[i], fr.at[i],
-            (mem, gx, lax.rem(gy_f + ngy, ngy)),
-        )
-
-    def direct_x():
-        return remote(xb.at[OWN], xb.at[par], ps.at[CHUNKS], pr.at[CHUNKS], (mem, gx, partner))
-
-    def arrival_x():
-        return remote(xb.at[OWN], xb.at[1 - par], ps.at[CHUNKS], pr.at[CHUNKS], (mem, gx, partner))
-
-    def forward_x():
-        return remote(
-            xb.at[1 - par], xb.at[par], fs.at[CHUNKS], fr.at[CHUNKS], (mem, gx, lax.rem(gy_f + ngy, ngy))
-        )
+    def half(h):
+        return pl.ds(pl.multiple_of(h * (CHUNK // 2), CHUNK // 2), CHUNK // 2)
+
+    def third(n):
+        return pl.ds(n * 128, 128)
+
+    after = (mem, gx, lax.rem(gy_f + ngy, ngy))
+
+    def direct(h):
+        return remote(own.at[half(h)], buf.at[par, half(h)], ps.at[h], pr.at[h], (mem, gx, partner))
+
+    def arrival(h):
+        return remote(own.at[half(h)], buf.at[1 - par, half(h)], ps.at[h], pr.at[h], (mem, gx, partner))
+
+    def forward(h):
+        return remote(buf.at[1 - par, half(h)], buf.at[par, half(h)], fs.at[h], fr.at[h], after)
+
+    def direct_x(n):
+        h = 2 * CHUNKS + n
+        return remote(xb.at[OWN, third(n)], xb.at[par, third(n)], ps.at[h], pr.at[h], (mem, gx, partner))
+
+    def arrival_x(n):
+        h = 2 * CHUNKS + n
+        return remote(xb.at[OWN, third(n)], xb.at[1 - par, third(n)], ps.at[h], pr.at[h], (mem, gx, partner))
+
+    def forward_x(n):
+        h = 2 * CHUNKS + n
+        return remote(xb.at[1 - par, third(n)], xb.at[par, third(n)], fs.at[h], fr.at[h], after)
 
     def issue(i):
         own[rows_of(i), :] = pert[rows_of(i), :].astype(f32)
-        direct(i).start()
+        direct(2 * i).start()
+        direct(2 * i + 1).start()
 
     def pump(i):
-        arrival(i).wait_recv()
-
-        @pl.when(has_f)
-        def _():
-            forward(i).start()
-
-        if isinstance(i, int) and i + AHEAD < CHUNKS:
+        for h in (2 * i, 2 * i + 1):
+            arrival(h).wait_recv()
+            pl.when(has_f)(lambda h=h: forward(h).start())
+        if i + AHEAD < CHUNKS:
             issue(i + AHEAD)
 
     def landed(i):
         @pl.when(has_b)
         def _():
-            forward(i).wait_recv()
+            forward(2 * i).wait_recv()
+            forward(2 * i + 1).wait_recv()
 
     for i in range(AHEAD):
         issue(i)
     fetch = pltpu.make_async_copy(alpha, work, al.at[0])
     fetch.start()
-
-    @pl.when(jnp.logical_not(has_b))
-    def _():
-        @pl.loop(0, CHUNKS)
-        def _(i):
-            buf[par, rows_of(i), :] = jnp.zeros((CHUNK, 128), f32)
-
-        xb[par] = jnp.zeros(xb.shape[1:], f32)
-
-    @pl.when(gx == 0)
-    def _():
-        side[0] = jnp.zeros(side.shape[1:], f32)
-        for it in range(ITERS):
-            mrecv[it, 0] = jnp.zeros(mrecv.shape[2:], f32)
-            for n in range(4):
-                nrecv[it, n, 0] = jnp.zeros((16, 128), f32)
-
-    @pl.when(gx == ngx - 1)
-    def _():
-        side[1] = jnp.zeros(side.shape[1:], f32)
-        for it in range(ITERS):
-            mrecv[it, 1] = jnp.zeros(mrecv.shape[2:], f32)
-            for n in range(4):
-                nrecv[it, n, 1] = jnp.zeros((16, 128), f32)
-
-    @pl.when(gy == 0)
-    def _():
-        f_dn[...] = jnp.zeros(f_dn.shape, f32)
-        g_dn[...] = jnp.zeros(g_dn.shape, f32)
-        for it in range(ITERS):
-            nrecv[it, 1] = jnp.zeros((2, 16, 128), f32)
-
-    @pl.when(gy < 2)
-    def _():
-        g_dn2[...] = jnp.zeros(g_dn2.shape, f32)
-        for it in range(ITERS):
-            nrecv[it, 3] = jnp.zeros((2, 16, 128), f32)
-
-    @pl.when(gy == ngy - 1)
-    def _():
-        f_up[...] = jnp.zeros(f_up.shape, f32)
-        g_up[...] = jnp.zeros(g_up.shape, f32)
-        for it in range(ITERS):
-            nrecv[it, 2] = jnp.zeros((2, 16, 128), f32)
-
-    @pl.when(gy >= ngy - 2)
-    def _():
-        f_up2[...] = jnp.zeros(f_up2.shape, f32)
 
     px, pa = iota((128, 128), 0), iota((128, 128), 1)
 
@@ -357,7 +316,73 @@
     pump(5)
     matrices(8, CHUNKS)
     pump(6)
+
+    @pl.when(jnp.logical_not(has_b))
+    def _():
+        @pl.loop(0, CHUNKS)
+        def _(i):
+            buf[par, rows_of(i), :] = jnp.zeros((CHUNK, 128), f32)
+
+        xb[par] = jnp.zeros(xb.shape[1:], f32)
+
+    @pl.when(gx == 0)
+    def _():
+        side[0] = jnp.zeros(side.shape[1:], f32)
+        for it in range(ITERS):
+            mrecv[it, 0] = jnp.zeros(mrecv.shape[2:], f32)
+            for n in range(4):
+                nrecv[it, n, 0] = jnp.zeros((16, 128), f32)
+
+    @pl.when(gx == ngx - 1)
+    def _():
+        side[1] = jnp.zeros(side.shape[1:], f32)
+        for it in range(ITERS):
+            mrecv[it, 1] = jnp.zeros(mrecv.shape[2:], f32)
+            for n in range(4):
+                nrecv[it, n, 1] = jnp.zeros((16, 128), f32)
+
+    @pl.when(gy == 0)
+    def _():
+        f_dn[...] = jnp.zeros(f_dn.shape, f32)
+        g_dn[...] = jnp.zeros(g_dn.shape, f32)
+        for it in range(ITERS):
+            nrecv[it, 1] = jnp.zeros((2, 16, 128), f32)
+
+    @pl.when(gy < 2)
+    def _():
+        g_dn2[...] = jnp.zeros(g_dn2.shape, f32)
+        for it in range(ITERS):
+            nrecv[it, 3] = jnp.zeros((2, 16, 128), f32)
+
+    @pl.when(gy == ngy - 1)
+    def _():
+        f_up[...] = jnp.zeros(f_up.shape, f32)
+        g_up[...] = jnp.zeros(g_up.shape, f32)
+        for it in range(ITERS):
+            nrecv[it, 2] = jnp.zeros((2, 16, 128), f32)
+
+    @pl.when(gy >= ngy - 2)
+    def _():
+        f_up2[...] = jnp.zeros(f_up2.shape, f32)
+
+    fetch.wait()
+    eb[...] = jnp.zeros(eb.shape, f32)
+    yh_s[...] = jnp.zeros(yh_s.shape, f32)
+
+    def lon(x, i):
+        hi, lo = split2(x)
+        return dot(jnp.concatenate([hi, lo], axis=1), wf[i, 0:256]) + dot(hi, wf[i, 256:384])
+
+    def lon_chunks(first, last):
+        @pl.loop(first, last)
+        def _(i):
+            wide = lon(work[rows_of(i), :], i)
+            y_all[rows_of(i), :] = wide[:, :128]
+            yh_s[:CHUNK] += wide[:, 128:]
+
+    lon_chunks(0, 8)
     pump(7)
+    lon_chunks(8, CHUNKS)
     for j in range(1, ngx):
         o1_in(j).wait_recv()
 
@@ -440,20 +465,16 @@
     def xb_rows(start):
         return [xb[b, every4(start + r), :] for b in (BELOW, OWN, ABOVE) for r in range(4)]
 
-    def lon(x, i):
-        hi, lo = split2(x)
-        return dot(jnp.concatenate([hi, lo], axis=1), wf[i, 0:256]) + dot(hi, wf[i, 256:384])
-
     def eb_at(row, c8):
         return pl.ds((row + 1) * 16 + c8 * 8, 8)
 
     def accumulate(parts, count):
         for c8 in range(2):
             acc = [eb[eb_at(row, c8), :] for row in range(12)]
-            for y, rows in parts:
+            for y, first, rows in parts:
                 for k in range(count):
                     start = k * 64 + c8 * 32
-                    z = lat_out([y[every4(start + r), :] for r in range(4)])
+                    z = lat_out([y[every4(first + start + r), :] for r in range(4)])
                     p = rows(start)
                     acc = [acc[row] + z[row] * p[row] for row in range(12)]
             for row in range(12):
@@ -471,13 +492,18 @@
             wide = lon(x, n)
             y[...] = wide[:, :128]
             yh_s[:CHUNK] += wide[:, 128:]
-        accumulate([(y_a, rows_from(i)), (y_b, rows_from(i + 1))], 4)
+        accumulate([(y_a, 0, rows_from(i)), (y_b, 0, rows_from(i + 1))], 4)
+
+    def arrived_pair(i):
+        landed(i)
+        landed(i + 1)
+        accumulate([(y_all, n * CHUNK, rows_from(n)) for n in (i, i + 1)], 4)
 
     def static_chunk(src):
         wide = lon(src[...] * jnp.where(mem == 0, 1.0, 0.0), 0)
         y_c[...] = wide[:, :128]
         yh_s[CHUNK:] = wide[:, 128:]
-        accumulate([(y_c, lambda start: xb_rows(320 + start))], 1)
+        accumulate([(y_c, 0, lambda start: xb_rows(320 + start))], 1)
 
     lane16 = iota((16, 128), 1)
     group16, place16 = lane16 >> 3, lane16 & 7
@@ -491,9 +517,7 @@
         s = s % 128
         return pltpu.roll(x, s, 1) if s else x
 
-    def reduce_and_observe(it):
-        whole = remote(eb.at[pl.ds(16, 192)], f_mem.at[it], bs.at[it, 0], br.at[it, 0], (1 - mem, gx, gy))
-        whole.start()
+    def halo_columns():
         for c8 in range(2):
             acc = [jnp.zeros((8, 128), f32) for _ in range(12)]
             for k in range(5):
@@ -504,12 +528,21 @@
             for row in range(12):
                 eh_s[row * 16 + c8 * 8 : row * 16 + c8 * 8 + 8] = acc[row]
         eh = around(eh_s[...])
-        halo, edge = jnp.zeros((16, 128), f32), jnp.zeros((16, 128), f32)
+        halo = jnp.zeros((16, 128), f32)
+        for row in range(12):
+            halo = jnp.where(group16 == row, eh[row * 16 : row * 16 + 16], halo)
+        msend[0:16] = halo
+
+    def reduce_and_observe(it):
+        whole = remote(eb.at[pl.ds(16, 192)], f_mem.at[it], bs.at[it, 0], br.at[it, 0], (1 - mem, gx, gy))
+        whole.start()
+        if it > 0:
+            halo_columns()
+        edge = jnp.zeros((16, 128), f32)
         for row in range(12):
             at = row * 16
-            halo = jnp.where(group16 == row, eh[at : at + 16], halo)
             edge = jnp.where(lane16 == 8 * row + 4, turn(eb[16 + at : 32 + at], 8 * row + 4), edge)
-        msend[0:16] = halo
+        halo = msend[0:16]
         msend[16:32] = edge
 
         def columns():
@@ -688,43 +721,33 @@
         gradient_rows([(y_c, lambda start: xb_rows(320 + start))], 1)
         stat_out[...] = (1.0 - DESCENT) * src[...] - (DESCENT * ENS) * gradient(y_c, CHUNK, 0)
 
-    clear()
-
-    fetch.wait()
     for i in range(8, CHUNKS):
         pump(i)
         if i == 8:
             finish_lon(to_right(pack.at[0], side.at[0], as_, ar), to_left(pack.at[1], side.at[1], as_, ar))
             xb[OWN, :320] = side[0] + side[1]
-            direct_x().start()
-        if i == 13:
-            arrival_x().wait_recv()
-
-            @pl.when(has_f)
-            def _():
-                forward_x().start()
-
-            for j in range(1, ngy):
-                o2_in(j).wait_recv()
-        if i >= 13 and i < 15:
-            operator(2 * i - 26)
-            operator(2 * i - 25)
-        if i < 15:
-
-            n = 2 * (i - 8)
-            landed(n)
-            landed(n + 1)
-            member_pair(n, [work[rows_of(n), :], work[rows_of(n + 1), :]])
-
-    landed(CHUNKS - 2)
-    landed(CHUNKS - 1)
-    member_pair(CHUNKS - 2, [work[rows_of(CHUNKS - 2), :], work[rows_of(CHUNKS - 1), :]])
+        if 8 <= i < 11:
+            direct_x(i - 8).start()
+        if 12 <= i < 15:
+            arrival_x(i - 12).wait_recv()
+            pl.when(has_f)(lambda i=i: forward_x(i - 12).start())
+        if i < 14:
+            arrived_pair(2 * (i - 8))
+
+    for j in range(1, ngy):
+        o2_in(j).wait_recv()
+    for q in range(4):
+        operator(q)
+    arrived_pair(CHUNKS - 4)
 
     @pl.when(has_b)
     def _():
-        forward_x().wait_recv()
+        for n in range(3):
+            forward_x(n).wait_recv()
 
     static_chunk(stat)
+    halo_columns()
+    arrived_pair(CHUNKS - 2)
     reduce_and_observe(0)
     clear()
 
@@ -746,15 +769,17 @@
     for i in range(CHUNKS):
         done(i).wait()
 
-    for i in range(CHUNKS):
-        direct(i).wait_send()
-    direct_x().wait_send()
+    for h in range(2 * CHUNKS):
+        direct(h).wait_send()
+    for n in range(3):
+        direct_x(n).wait_send()
 
     @pl.when(has_f)
     def _():
-        for i in range(CHUNKS):
-            forward(i).wait_send()
-        forward_x().wait_send()
+        for h in range(2 * CHUNKS):
+            forward(h).wait_send()
+        for n in range(3):
+            forward_x(n).wait_send()
 
     for j in range(1, ngx):
         o1(j).wait_send()
@@ -804,6 +829,7 @@
         V((2, 320, 128), f32),
         V((CHUNKS, 384, 256), bf16),
         V((CHUNKS, 256, 256), bf16),
+        V((rows, 128), f32),
         V((CHUNK, 128), f32),
         V((CHUNK, 128), f32),
         V((64, 128), f32),
@@ -835,7 +861,7 @@
         V((8, 2048), f32),
         V((160, 256), bf16),
         V((160, 128), f32),
-        dma((CHUNKS + 1,)), dma((CHUNKS + 1,)), dma((CHUNKS + 1,)), dma((CHUNKS + 1,)),
+        dma((2 * CHUNKS + 3,)), dma((2 * CHUNKS + 3,)), dma((2 * CHUNKS + 3,)), dma((2 * CHUNKS + 3,)),
         dma((2,)), dma((2,)),
         dma((8,)), dma((8,)), dma((8,)), dma((8,)),
         dma((ITERS, 5)), dma((ITERS, 5)),

time: 122 us -> 120 us (0.984)
  Pallas kernels: 122 us -> 119 us
    pallas_call x1, Pallas kernels: 119 us -> 116 us  [per_device(): pl.pallas_call(body, out_shape=(jax.ShapeDtypeStruct((rows, 128), f32), j...]
where the time goes in v5:
time: 120 us; the launch traced here: 119 us
  Pallas kernels  119 us (99%)
    pallas_call x1, Pallas kernels, per_device(): pl.pallas_call(body, out_shape=(jax.ShapeDtypeStruct((rows, 128), f32), j...  116 us
    pallas_call x1, Pallas kernels, per_device(): pl.pallas_call(hand_over, out_shape=tuple((jax.ShapeDtypeStruct(x.shape,...  2.44 us

profile of v5, /device:TPU:1, one launch (start us, length us, event | category | flops | bytes accessed | tf_op | source)
XLA Modules:
  0.0 119.5 jit_solution(17564661530132511603)
XLA Ops:
  0.6 116.4 %assimilate.1 = (f32[4096,128]{1,0:T(8,128)}, f32[64,128]{1,0:T(8,128)}, f32[64,128]{1,0:T(8,128)}) custom-call(f32[4096,128]{1,0:T(8,128)} %bitcast.12, bf16[4096,128]{1,0:T(8,128)(2,1)} %bitcast.13, f32[64,128]{1,0:T(8,128)} %bitcast.15, f32[64,128]{1,0:T(8,128)} %bitcast.16, f32[16,1024]{1,0:T(8,128)} %bitcast.14, f32[4,1024]{1,0:T(4,128)} %interp.1, ...), custom_call_target="tpu_custom_call" | custom-call | tf_op jit(solution)/shard_map/assimilate/pallas_call | solution.py:873
  117.0 2.4 %hand_over.1 = (f32[4096,128]{1,0:T(8,128)}, f32[64,128]{1,0:T(8,128)}, f32[64,128]{1,0:T(8,128)}) custom-call(f32[4096,128]{1,0:T(8,128)} %get-tuple-element.9.a, f32[64,128]{1,0:T(8,128)} %get-tuple-element.10.b, f32[64,128]{1,0:T(8,128)} %get-tuple-element.11.c), custom_call_target="tpu_custom_call" | custom-call | tf_op jit(solution)/shard_map/hand_over/pallas_call | solution.py:889

commit v6 on v5

--- a/solution.py
+++ b/solution.py
@@ -125,7 +125,7 @@
         return pl.ds(pl.multiple_of(h * (CHUNK // 2), CHUNK // 2), CHUNK // 2)
 
     def third(n):
-        return pl.ds(n * 128, 128)
+        return pl.ds(n * 128, 128 if n < 2 else 72)
 
     after = (mem, gx, lax.rem(gy_f + ngy, ngy))
 
@@ -174,6 +174,12 @@
     fetch.start()
 
     px, pa = iota((128, 128), 0), iota((128, 128), 1)
+    own_group = (iota((16, 128), 1) >> 3) == iota((16, 128), 0)
+
+    def around(x):
+        for s in (8, 16, 32, 64):
+            x = x + pltpu.roll(x, s, 1)
+        return x
 
     tri = jnp.where(px < pa, 1.0, 0.0).astype(bf16)
     totals = jnp.zeros((64, 1), f32)
@@ -245,12 +251,16 @@
         pack[1, :CHUNK] += picked[:, 128:]
 
     scaled = sig[...] * (STATIC / ENS)
-    xb[OWN, 320:384] = scaled
+    xb[OWN, 256:320] = scaled
     hi, mid, lo = split3(scaled)
     sel = selection(0)
     picked = dot(hi, sel) + dot(mid, sel) + dot(lo, sel)
-    pack[0, CHUNK:] = picked[:, :128]
-    pack[1, CHUNK:] = picked[:, 128:]
+    for n in range(2):
+        y_c[...] = picked[:, n * 128 : (n + 1) * 128]
+        for r in range(4):
+            x = jnp.concatenate([y_c[pl.ds(r, 8, stride=4), :], y_c[pl.ds(32 + r, 8, stride=4), :]], axis=0)
+            x = jnp.where(own_group, around(x), 0.0)
+            pack[n, CHUNK + r : CHUNK + r + 1] = jnp.sum(x, axis=0, keepdims=True)
 
     right, left = lax.rem(gx + 1, ngx), lax.rem(gx + ngx - 1, ngx)
 
@@ -503,15 +513,10 @@
         wide = lon(src[...] * jnp.where(mem == 0, 1.0, 0.0), 0)
         y_c[...] = wide[:, :128]
         yh_s[CHUNK:] = wide[:, 128:]
-        accumulate([(y_c, 0, lambda start: xb_rows(320 + start))], 1)
+        accumulate([(y_c, 0, lambda start: xb_rows(256 + start))], 1)
 
     lane16 = iota((16, 128), 1)
     group16, place16 = lane16 >> 3, lane16 & 7
-
-    def around(x):
-        for s in (8, 16, 32, 64):
-            x = x + pltpu.roll(x, s, 1)
-        return x
 
     def turn(x, s):
         s = s % 128
@@ -523,7 +528,7 @@
             for k in range(5):
                 start = k * 64 + c8 * 32
                 z = lat_out([yh_s[every4(start + r), :] for r in range(4)])
-                p = xb_rows(start)
+                p = xb_rows(start if k < 4 else 328 + c8 * 32)
                 acc = [acc[row] + z[row] * p[row] for row in range(12)]
             for row in range(12):
                 eh_s[row * 16 + c8 * 8 : row * 16 + c8 * 8 + 8] = acc[row]
@@ -671,7 +676,7 @@
             g = [gh_s[row * 16 + c8 * 8 : row * 16 + c8 * 8 + 8] for row in range(12)]
             for k in range(5):
                 start = k * 64 + c8 * 32
-                p = xb_rows(start)
+                p = xb_rows(start if k < 4 else 328 + c8 * 32)
                 v = lat_in([p[row] * g[row] for row in range(12)])
                 for r in range(4):
                     yh_s[every4(start + r), :] = v[r]
@@ -718,14 +723,15 @@
         return pltpu.make_async_copy(work.at[rows_of(i)], alpha_out.at[rows_of(i)], ao.at[i])
 
     def static_step(src):
-        gradient_rows([(y_c, lambda start: xb_rows(320 + start))], 1)
+        gradient_rows([(y_c, lambda start: xb_rows(256 + start))], 1)
         stat_out[...] = (1.0 - DESCENT) * src[...] - (DESCENT * ENS) * gradient(y_c, CHUNK, 0)
 
     for i in range(8, CHUNKS):
         pump(i)
         if i == 8:
             finish_lon(to_right(pack.at[0], side.at[0], as_, ar), to_left(pack.at[1], side.at[1], as_, ar))
-            xb[OWN, :320] = side[0] + side[1]
+            xb[OWN, :256] = side[0, :256] + side[1, :256]
+            xb[OWN, 320:328] = side[0, 256:264] + side[1, 256:264]
         if 8 <= i < 11:
             direct_x(i - 8).start()
         if 12 <= i < 15:
@@ -745,6 +751,11 @@
         for n in range(3):
             forward_x(n).wait_recv()
 
+    for b in (BELOW, OWN, ABOVE):
+        for r in range(4):
+            x = around(jnp.where(own_group, xb[b, 320 + r : 321 + r], 0.0))
+            xb[b, every4(328 + r), :] = x[:8]
+            xb[b, every4(360 + r), :] = x[8:]
     static_chunk(stat)
     halo_columns()
     arrived_pair(CHUNKS - 2)
@@ -824,9 +835,9 @@
         V((rows, 128), f32),
         V((rows, 128), f32),
         V((2, rows, 128), f32),
-        V((3, 384, 128), f32),
-        V((2, 320, 128), f32),
-        V((2, 320, 128), f32),
+        V((3, 392, 128), f32),
+        V((2, 264, 128), f32),
+        V((2, 264, 128), f32),
         V((CHUNKS, 384, 256), bf16),
         V((CHUNKS, 256, 256), bf16),
         V((rows, 128), f32),

time: 120 us -> 119 us (level)
  no operation moved by 1% of the time
where the time goes in v6:
time: 119 us
  Pallas kernels  119 us (100%)
    pallas_call x1, Pallas kernels, per_device(): pl.pallas_call(body, out_shape=(jax.ShapeDtypeStruct((rows, 128), f32), j...  116 us
    pallas_call x1, Pallas kernels, per_device(): pl.pallas_call(hand_over, out_shape=tuple((jax.ShapeDtypeStruct(x.shape,...  2.44 us

profile of v6, /device:TPU:1, one launch (start us, length us, event | category | flops | bytes accessed | tf_op | source)
XLA Modules:
  0.0 119.2 jit_solution(12484221567514974758)
XLA Ops:
  0.6 116.1 %assimilate.1 = (f32[4096,128]{1,0:T(8,128)}, f32[64,128]{1,0:T(8,128)}, f32[64,128]{1,0:T(8,128)}) custom-call(f32[4096,128]{1,0:T(8,128)} %bitcast.12, bf16[4096,128]{1,0:T(8,128)(2,1)} %bitcast.13, f32[64,128]{1,0:T(8,128)} %bitcast.15, f32[64,128]{1,0:T(8,128)} %bitcast.16, f32[16,1024]{1,0:T(8,128)} %bitcast.14, f32[4,1024]{1,0:T(4,128)} %interp.1, ...), custom_call_target="tpu_custom_call" | custom-call | tf_op jit(solution)/shard_map/assimilate/pallas_call | solution.py:884
  116.8 2.4 %hand_over.1 = (f32[4096,128]{1,0:T(8,128)}, f32[64,128]{1,0:T(8,128)}, f32[64,128]{1,0:T(8,128)}) custom-call(f32[4096,128]{1,0:T(8,128)} %get-tuple-element.9.a, f32[64,128]{1,0:T(8,128)} %get-tuple-element.10.b, f32[64,128]{1,0:T(8,128)} %get-tuple-element.11.c), custom_call_target="tpu_custom_call" | custom-call | tf_op jit(solution)/shard_map/hand_over/pallas_call | solution.py:900
